TPU v7x, 32 devices: a whole 2x2x4 slice. The times are simulated.
32 devices in a mesh: gx: 8 (over z, y), gy: 4 (over x, core).
Axes of the slice: x: 2, y: 2, z: 4, core: 2. Of those that a mesh axis runs over, the one named last changes fastest.
Arguments:
- density: float32 [1, 512, 2048], P(None, 'gy', 'gx'), may hold values from 0.5 to 4
- velocity: float32 [2, 1, 512, 2048], P(None, None, 'gy', 'gx'), may hold values from -1 to 1
- energy: float32 [1, 512, 2048], P(None, 'gy', 'gx'), may hold values from 0.5 to 3
- material: int32 [1, 512, 2048], P(None, 'gy', 'gx'), may hold values from 0 to 2
- limiter: int32 [1, 512, 2048], P(None, 'gy', 'gx'), may hold values 0 or 1
- owners: int32 [8192], P(('gx', 'gy')), may hold values from 0 to 7, as said below
- dest_tile: int32 [8192], P(('gx', 'gy')), may hold values from 0 to 255, as said below
- tile_shift: float32 [1, 512], P(None, 'gy'), may hold values from 0.25 to 0.75
Outputs:
- remapped: float32 [4, 1, 512, 2048], P(None, None, 'gy', 'gx')
Inputs may be any that keep to these rules, and one draw needn't show every extreme that they name: `owners`: within a plane every mesh row of tiles is rotated along x as a whole by a whole number of tiles, at most 1 either way, and the rotation does not fall from one row to the next; so a tile's owner is its own gx index or the one next to it on either side (wrapping). No device sends more than 128 tiles to either neighbour, and in every draw some device sends exactly 128 to its left neighbour and some exactly 128 to its right one. `dest_tile`: numbered like the owner's own tiles; a destination lies in the tile's own plane and row, and every Eulerian tile is the destination of exactly one Lagrangian tile.
All inputs are finite; a program needn't handle non-finite values. No bound on the sum of `limiter` on one device may be relied on, other than what follows from the above.
Results may differ from a plain program's by a relative error of at most 0.0003.
Values sent between devices are 32-bit elements; how exact they have to be, the bound alone decides.
No kernel may reach another device: no remote copies, remote signals or barrier semaphores. Data moves between devices by JAX's collectives and lax.ppermute only.
A program may use at most 64 MiB of HBM per device.

v0:
```python
import jax
import jax.numpy as jnp
from jax import lax
from jax.sharding import PartitionSpec as P

TILE = 128


time_step = 0.05


def padded_2(cells, sides, width):
    for axis, dim in sides:
        count = lax.axis_size(axis)
        head = lax.slice_in_dim(cells, 0, width, axis=dim)
        tail = lax.slice_in_dim(cells, cells.shape[dim] - width, cells.shape[dim], axis=dim)
        cells = jnp.concatenate(
            [
                lax.ppermute(tail, axis, [(i, (i + 1) % count) for i in range(count)]),
                cells,
                lax.ppermute(head, axis, [((i + 1) % count, i) for i in range(count)]),
            ],
            axis=dim,
        )
    return cells


def passed_along(value, axis, steps):
    count = lax.axis_size(axis)
    pairs = [(source, (source + steps) % count) for source in range(count)]
    return lax.ppermute(value, axis, pairs)


def heat_ratio(material):
    return jnp.where(material == 0, 1.4, jnp.where(material == 1, 5.0 / 3.0, 3.0)).astype(
        jnp.float32
    )


def corners(grid_field):
    return (
        grid_field[..., :-1, :-1],
        grid_field[..., :-1, 1:],
        grid_field[..., 1:, :-1],
        grid_field[..., 1:, 1:],
    )


def node_velocity(impedance, pressure, speed_x, speed_y):
    weights = corners(impedance)
    pushes = corners(pressure)
    along_x = corners(speed_x)
    along_y = corners(speed_y)
    totals = weights[0] + weights[1] + weights[2] + weights[3]
    moment_x = (
        weights[0] * along_x[0]
        + weights[1] * along_x[1]
        + weights[2] * along_x[2]
        + weights[3] * along_x[3]
    )
    moment_y = (
        weights[0] * along_y[0]
        + weights[1] * along_y[1]
        + weights[2] * along_y[2]
        + weights[3] * along_y[3]
    )
    node_x = (moment_x + (pushes[0] - pushes[1] + pushes[2] - pushes[3])) / totals
    node_y = (moment_y + (pushes[0] + pushes[1] - pushes[2] - pushes[3])) / totals
    return (node_x, node_y)


def cell_update(impedance, pressure, speed_x, speed_y, density, energy_total, node_x, node_y):
    nodes_x = corners(node_x)
    nodes_y = corners(node_y)
    sum_x = nodes_x[0] + nodes_x[1] + nodes_x[2] + nodes_x[3]
    sum_y = nodes_y[0] + nodes_y[1] + nodes_y[2] + nodes_y[3]
    force_x = 0.5 * impedance * (sum_x - 4.0 * speed_x)
    force_y = 0.5 * impedance * (sum_y - 4.0 * speed_y)
    volume_rate = 0.5 * (
        -nodes_x[0]
        - nodes_y[0]
        + nodes_x[1]
        - nodes_y[1]
        - nodes_x[2]
        + nodes_y[2]
        + nodes_x[3]
        + nodes_y[3]
    )
    relaxation = jnp.zeros_like(speed_x)
    for corner in range(4):
        relaxation = (
            relaxation
            + (nodes_x[corner] - speed_x) * nodes_x[corner]
            + (nodes_y[corner] - speed_y) * nodes_y[corner]
        )
    work_rate = -pressure * volume_rate + 0.5 * impedance * relaxation
    conserved = jnp.stack(
        [
            density,
            density * speed_x + time_step * force_x,
            density * speed_y + time_step * force_y,
            energy_total + time_step * work_rate,
        ]
    )
    left_speed = 0.5 * (nodes_x[0] + nodes_x[2])
    right_speed = 0.5 * (nodes_x[1] + nodes_x[3])
    widths = 1.0 + time_step * (right_speed - left_speed)
    return (conserved / widths, left_speed, right_speed)


def minmod(left_side, right_side):
    return jnp.where(
        left_side * right_side > 0,
        jnp.sign(left_side) * jnp.minimum(jnp.abs(left_side), jnp.abs(right_side)),
        0.0,
    )


def centred(left_side, right_side):
    limit_mag = jnp.minimum(
        jnp.minimum(2.0 * jnp.abs(left_side), 2.0 * jnp.abs(right_side)),
        0.5 * jnp.abs(left_side + right_side),
    )
    return jnp.where(left_side * right_side > 0, jnp.sign(left_side) * limit_mag, 0.0)


def limited(values, neighbour_left, neighbour_right, limiter):
    widened = jnp.concatenate([neighbour_left, values, neighbour_right], axis=-1)
    back_diff = values - widened[..., :-2]
    fore_diff = widened[..., 2:] - values
    return jnp.where(limiter == 1, centred(back_diff, fore_diff), minmod(back_diff, fore_diff))


def integrate(values, slopes, left_pos, right_pos):
    cell_pos = jnp.arange(values.shape[-1]).astype(jnp.float32)
    centre = 0.5 * (left_pos + right_pos)
    low_own = jnp.maximum(left_pos, cell_pos)
    high_own = jnp.minimum(right_pos, cell_pos + 1.0)
    span_own = jnp.maximum(high_own - low_own, 0.0)
    offset_own = 0.5 * (high_own + low_own) - centre
    low_next = jnp.maximum(left_pos, cell_pos + 1.0)
    high_next = jnp.minimum(right_pos, cell_pos + 2.0)
    span_next = jnp.maximum(high_next - low_next, 0.0)
    offset_next = 0.5 * (high_next + low_next) - centre
    part_own = span_own[..., None, :] * (values + slopes * offset_own[..., None, :])
    part_next = span_next[..., None, :] * (values + slopes * offset_next[..., None, :])
    empty_col = jnp.zeros_like(part_next[..., :1])
    main_part = part_own + jnp.concatenate([empty_col, part_next[..., :-1]], axis=-1)
    return (main_part, part_next[..., -1])


def wall_rows(padded, width):
    level = lax.axis_index("gy")
    row_total = padded.shape[2]
    row_index = jnp.arange(row_total)
    outside = (row_index < width) & (level == 0) | (row_index >= row_total - width) & (
        level == lax.axis_size("gy") - 1
    )
    return jnp.where(outside[:, None], 0.0, padded)


def on_device(density, velocity, energy, material, limiter, owners, dest_tile, tile_shift):
    planes, rows_dev, cols_dev = density.shape
    segments = cols_dev // TILE
    tile_count = planes * rows_dev * segments
    row_count = planes * rows_dev
    capacity = tile_count // 2
    ratios = heat_ratio(material)
    pressure = (ratios - 1.0) * density * energy
    impedance = density * jnp.sqrt(ratios * (ratios - 1.0) * energy)
    speed_x = velocity[0]
    speed_y = velocity[1]
    energy_total = density * (energy + 0.5 * (speed_x * speed_x + speed_y * speed_y))
    padded = padded_2(jnp.stack([impedance, pressure, speed_x, speed_y]), (("gx", 3), ("gy", 2)), 1)
    padded = wall_rows(padded, 1)
    node_x, node_y = node_velocity(padded[0], padded[1], padded[2], padded[3])
    values, left_speed, right_speed = cell_update(
        impedance, pressure, speed_x, speed_y, density, energy_total, node_x, node_y
    )
    rim_cells = padded_2(values, (("gx", 3),), 1)
    neighbour_left = rim_cells[..., :1]
    neighbour_right = rim_cells[..., -1:]
    slopes = limited(values, neighbour_left, neighbour_right, limiter)
    tile_values = values.reshape(4, tile_count, TILE).transpose(1, 0, 2)
    tile_slopes = slopes.reshape(4, tile_count, TILE).transpose(1, 0, 2)
    cell_pos = jnp.arange(TILE).astype(jnp.float32)
    offsets = jnp.broadcast_to(tile_shift[:, :, None], (planes, rows_dev, segments)).reshape(
        tile_count, 1
    )
    left_pos = cell_pos + offsets + time_step * left_speed.reshape(tile_count, TILE)
    right_pos = cell_pos + 1.0 + offsets + time_step * right_speed.reshape(tile_count, TILE)
    column = lax.axis_index("gx")
    col_count = lax.axis_size("gx")
    step_over = (owners - column) % col_count
    go_right = step_over == 1
    go_left = step_over == col_count - 1
    stays_home = step_over == 0
    rank_left = jnp.cumsum(go_left.astype(jnp.int32)) - 1
    rank_right = jnp.cumsum(go_right.astype(jnp.int32)) - 1
    slot_ids = jnp.where(
        go_left, rank_left, jnp.where(go_right, capacity + rank_right, 2 * capacity)
    )
    label_values = dest_tile.astype(jnp.float32)
    main_part, spill_part = integrate(tile_values, tile_slopes, left_pos, right_pos)
    extra_row = jnp.concatenate(
        [spill_part, label_values[:, None], jnp.zeros((tile_count, TILE - 5), jnp.float32)], axis=1
    )
    packet = jnp.concatenate([main_part, extra_row[:, None, :]], axis=1)
    send_buffer = (
        jnp.zeros((2 * capacity + 1, 5, TILE), jnp.float32).at[slot_ids].set(packet)[: 2 * capacity]
    )
    widened = padded_2(send_buffer, (("gx", 0),), capacity)
    incoming = jnp.concatenate([widened[:capacity], widened[3 * capacity :]], axis=0)
    incoming_main = incoming[:, 0:4]
    incoming_spill = incoming[:, 4, 0:4]
    incoming_labels = incoming[:, 4, 4]
    local_targets = jnp.where(stays_home, dest_tile, tile_count)
    all_targets = jnp.concatenate([local_targets, incoming_labels.astype(jnp.int32)])
    all_main = jnp.concatenate([main_part, incoming_main], axis=0)
    all_spill = jnp.concatenate([spill_part, incoming_spill], axis=0)
    gathered = jax.ops.segment_sum(all_main, all_targets, num_segments=tile_count + 1)[:tile_count]
    is_valid = all_targets < tile_count
    at_end = all_targets % segments == segments - 1
    inside_targets = jnp.where(is_valid & jnp.logical_not(at_end), all_targets + 1, tile_count)
    edge_targets = jnp.where(is_valid & at_end, all_targets // segments, row_count)
    inside = jax.ops.segment_sum(all_spill, inside_targets, num_segments=tile_count + 1)[
        :tile_count
    ]
    edge_spill = jax.ops.segment_sum(all_spill, edge_targets, num_segments=row_count + 1)[
        :row_count
    ]
    arrived = passed_along(edge_spill.T, "gx", 1)
    entering = jnp.concatenate(
        [arrived.T[:, None, :], jnp.zeros((row_count, segments - 1, 4), jnp.float32)], axis=1
    ).reshape(tile_count, 4)
    result = gathered.at[:, :, 0].add(inside + entering)
    return result.transpose(1, 0, 2).reshape(4, planes, rows_dev, cols_dev)


def solution(mesh):
    placed = (
        P(None, "gy", "gx"),
        P(None, None, "gy", "gx"),
        P(None, "gy", "gx"),
        P(None, "gy", "gx"),
        P(None, "gy", "gx"),
        P(("gx", "gy")),
        P(("gx", "gy")),
        P(None, "gy"),
    )
    return jax.shard_map(
        on_device, mesh=mesh, in_specs=placed, out_specs=P(None, None, "gy", "gx"), check_vma=False
    )
```

profile of v0, /device:TPU:0, one launch (start us, length us, event | category | flops | bytes accessed | tf_op | source)
XLA Modules:
  0.0 115.8 jit_solution(12325349105319710550)
XLA Ops:
  0.0 1.2 %fusion.48 = (f32[1,1,128,256]{3,2,1,0:T(8,128)S(1)}, pred[1,128,256]{2,1,0:T(8,128)(4,1)S(1)}, pred[1,128,256]{2,1,0:T(8,128)(4,1)S(1)}) fusion(f32[1,128,256]{2,1,0:T(8,128)} %param.10, f32[1,128,256]{2,1,0:T(8,128)} %param.12, s32[1,128,256]{2,1,0:T(8,128)} %param.13), kind=kLoop, calls=%fused_computation.148 | loop fusion | flops 262144 | bytes 589824 | tf_op jit(solution)/shard_map/stack | solution.py:174
  1.2 1.0 fusion.43
  2.4 3.0 %collective-permute-start = (f32[4,1,128,1]{3,2,1,0:T(8,128)S(1)}, f32[4,1,128,1]{3,2,1,0:T(8,128)S(1)}, u32[]{:S(2)}, u32[]{:S(2)}) collective-permute-start(f32[4,1,128,1]{3,2,1,0:T(8,128)S(1)} %get-tuple-element.34), channel_id=1, source_target_pairs={{0,4},{4,8},{8,12},{12,16},{16,20},{20,24},{24,28},{28,0},{1,5},{5... | collective-permute-start | bytes 6152 | tf_op jit(solution)/shard_map/ppermute | solution.py:19
  5.5 3.1 %collective-permute-start.1 = (f32[4,1,128,1]{3,2,1,0:T(8,128)S(1)}, f32[4,1,128,1]{3,2,1,0:T(8,128)S(1)}, u32[]{:S(2)}, u32[]{:S(2)}) collective-permute-start(f32[4,1,128,1]{3,2,1,0:T(8,128)S(1)} %get-tuple-element.35), channel_id=1, source_target_pairs={{4,0},{8,4},{12,8},{16,12},{20,16},{24,20},{28,24},{0,28},{5,1},{9... | collective-permute-start | bytes 6152 | tf_op jit(solution)/shard_map/ppermute | solution.py:21
  9.7 6.9 %collective-permute-done = f32[4,1,128,1]{3,2,1,0:T(8,128)S(1)} collective-permute-done((f32[4,1,128,1]{3,2,1,0:T(8,128)S(1)}, f32[4,1,128,1]{3,2,1,0:T(8,128)S(1)}, u32[]{:S(2)}, u32[]{:S(2)}) %collective-permute-start) | collective-permute-done | bytes 2080 | tf_op jit(solution)/shard_map/ppermute | solution.py:19
  16.7 2.2 %collective-permute-done.1 = f32[4,1,128,1]{3,2,1,0:T(8,128)S(1)} collective-permute-done((f32[4,1,128,1]{3,2,1,0:T(8,128)S(1)}, f32[4,1,128,1]{3,2,1,0:T(8,128)S(1)}, u32[]{:S(2)}, u32[]{:S(2)}) %collective-permute-start.1) | collective-permute-done | bytes 2080 | tf_op jit(solution)/shard_map/ppermute | solution.py:21
  19.0 1.7 %collective-permute-start.3 = (f32[4,1,1,258]{3,2,1,0:T(1,128)S(1)}, f32[4,1,1,258]{3,2,1,0:T(1,128)S(1)}, u32[]{:S(2)}, u32[]{:S(2)}) collective-permute-start(f32[4,1,1,258]{3,2,1,0:T(1,128)S(1)} %get-tuple-element.25), channel_id=1, source_target_pairs={{1,0},{2,1},{3,2},{0,3},{5,4},{6,5},{7,6},{4,7},{9,8},{10,9},{11,1... | collective-permute-start | bytes 12392 | tf_op jit(solution)/shard_map/ppermute | solution.py:21
  21.3 0.8 collective-permute-done.2
  22.1 0.4 maximum_select_fusion
  22.6 0.4 fusion.6
  23.0 0.5 copy-done.2
  23.6 0.4 fusion.11
  24.1 0.4 fusion.39
  24.8 0.8 fusion.50
  25.9 4.4 %collective-permute-start.5 = (f32[4,1,128,1]{3,2,1,0:T(8,128)}, f32[4,1,128,1]{3,2,1,0:T(8,128)S(1)}, u32[]{:S(2)}, u32[]{:S(2)}) collective-permute-start(f32[4,1,128,1]{3,2,1,0:T(8,128)} %get-tuple-element.32), channel_id=1, source_target_pairs={{4,0},{8,4},{12,8},{16,12},{20,16},{24,20},{28,24},{0,28},{5,1},{9... | collective-permute-start | bytes 6152 | tf_op jit(solution)/shard_map/ppermute | solution.py:21
  30.6 7.4 %collective-permute-done.4 = f32[4,1,128,1]{3,2,1,0:T(8,128)S(1)} collective-permute-done((f32[4,1,128,1]{3,2,1,0:T(8,128)}, f32[4,1,128,1]{3,2,1,0:T(8,128)S(1)}, u32[]{:S(2)}, u32[]{:S(2)}) %collective-permute-start.4) | collective-permute-done | bytes 2080 | tf_op jit(solution)/shard_map/ppermute | solution.py:19
  37.9 2.8 %collective-permute-done.5 = f32[4,1,128,1]{3,2,1,0:T(8,128)S(1)} collective-permute-done((f32[4,1,128,1]{3,2,1,0:T(8,128)}, f32[4,1,128,1]{3,2,1,0:T(8,128)S(1)}, u32[]{:S(2)}, u32[]{:S(2)}) %collective-permute-start.5) | collective-permute-done | bytes 2080 | tf_op jit(solution)/shard_map/ppermute | solution.py:21
  40.7 0.6 select_select_fusion
  41.4 0.8 multiply_bitcast_fusion
  42.2 0.3 slice.273
  42.9 0.9 bitcast_add_fusion
  44.2 7.2 %scatter_fusion = f32[257,5,128]{2,1,0:T(8,128)S(1)} fusion(f32[257,5,128]{2,1,0:T(8,128)S(1)} %broadcast_in_dim.97, s32[256]{0:T(256)S(1)} %compare_select_fusion.3, f32[256,5,128]{2,1,0:T(8,128)S(1)} %pad_maximum_fusion), kind=kCustom, calls=%fused_computation | custom fusion | bytes 1967104 | tf_op jit(solution)/shard_map/scatter | solution.py:210
  51.6 4.7 %collective-permute-start.7 = (f32[128,5,128]{2,1,0:T(8,128)S(1)}, f32[128,5,128]{2,1,0:T(8,128)S(1)}, u32[]{:S(2)}, u32[]{:S(2)}) collective-permute-start(f32[128,5,128]{2,1,0:T(8,128)S(1)} %get-tuple-element.22), channel_id=1, source_target_pairs={{4,0},{8,4},{12,8},{16,12},{20,16},{24,20},{28,24},{0,28},{5,1},{9... | collective-permute-start | bytes 983048 | tf_op jit(solution)/shard_map/ppermute | solution.py:21
  56.3 18.6 %collective-permute-done.6 = f32[128,5,128]{2,1,0:T(8,128)S(1)} collective-permute-done((f32[128,5,128]{2,1,0:T(8,128)S(1)}, f32[128,5,128]{2,1,0:T(8,128)S(1)}, u32[]{:S(2)}, u32[]{:S(2)}) %collective-permute-start.6) | collective-permute-done | bytes 327712 | tf_op jit(solution)/shard_map/ppermute | solution.py:19
  74.9 3.3 %collective-permute-done.7 = f32[128,5,128]{2,1,0:T(8,128)S(1)} collective-permute-done((f32[128,5,128]{2,1,0:T(8,128)S(1)}, f32[128,5,128]{2,1,0:T(8,128)S(1)}, u32[]{:S(2)}, u32[]{:S(2)}) %collective-permute-start.7) | collective-permute-done | bytes 327712 | tf_op jit(solution)/shard_map/ppermute | solution.py:21
  78.4 5.0 %fusion.30 = s32[256]{0:T(256)S(1)} fusion(f32[256,5,128]{2,1,0:T(8,128)S(1)} %constant_dynamic-update-slice_fusion), kind=kLoop, calls=%fused_computation.74 | loop fusion | flops 256 | bytes 2048 | tf_op jit(solution)/shard_map/convert_element_type | solution.py:218
  83.5 3.6 %scatter_custom_fusion.3 = f32[129,4]{1,0:T(8,128)S(1)} fusion(s32[512]{0:T(512)S(1)} %bitcast.118, f32[256,4]{1,0:T(8,128)S(1)} %bitcast.105, f32[]{:T(128)} %constant.148, f32[256,4]{1,0:T(8,128)S(1)} %copy.119, f32[]{:T(128)} %constant.114.clone.1), kind=kCustom, calls=%fused_computation.21 | custom fusion | flops 4096 | bytes 264216 | tf_op jit(solution)/shard_map/scatter-add | solution.py:229
  87.5 3.5 %scatter_custom_fusion.2 = f32[257,4]{1,0:T(8,128)S(1)} fusion(s32[512]{0:T(512)S(1)} %bitcast.117, f32[256,4]{1,0:T(8,128)S(1)} %bitcast.106, f32[]{:T(128)} %constant.148, f32[256,4]{1,0:T(8,128)S(1)} %copy.119, f32[]{:T(128)} %constant.114.clone.1), kind=kCustom, calls=%fused_computation.22 | custom fusion | flops 4096 | bytes 266264 | tf_op jit(solution)/shard_map/scatter-add | solution.py:226
  91.1 17.3 %scatter_fusion.1 = f32[257,4,128]{2,1,0:T(4,128)S(1)} fusion(f32[257,4,128]{2,1,0:T(4,128)S(1)} %broadcast_in_dim.95, s32[512]{0:T(512)S(1)} %pad_add_fusion, f32[512,4,128]{2,1,0:T(4,128)S(1)} %pad_maximum_fusion.1), kind=kCustom, calls=%fused_computation.1 | custom fusion | flops 262144 | bytes 3147776 | tf_op jit(solution)/shard_map/scatter-add | solution.py:221
  108.7 1.7 %copy.126 = f32[256,4,1]{2,1,0:T(4,128)S(1)} copy(f32[256,4,1]{1,0,2:T(8,128)S(1)} %fusion.29) | data formatting | bytes 8192 | tf_op jit(solution)/shard_map/reshape.30
  110.5 4.3 %scatter-add.29 = f32[256,4,128]{2,1,0:T(4,128)S(1)} dynamic-update-slice(f32[256,4,128]{2,1,0:T(4,128)S(1)} %slice.278, f32[256,4,1]{2,1,0:T(4,128)S(1)} %slice_add_fusion, s32[]{:T(128)} %constant.117.clone.1, s32[]{:T(128)} %constant.117.clone.1, s32[]{:T(128)} %constant.117.clone.1) | dynamic-update-slice | bytes 8196 | tf_op jit(solution)/shard_map/scatter-add | solution.py:236
  114.9 0.9 reshape.879
  (77 shorter events, 5.0 us)
Async XLA Ops:
  0.0 2.2 %copy-start = (f32[2,1,128,256]{3,2,1,0:T(8,128)S(1)}, f32[2,1,128,256]{3,2,1,0:T(8,128)}, u32[]{:S(2)}) copy-start(f32[2,1,128,256]{3,2,1,0:T(8,128)} %param.11) | copy-start | bytes 786436
  2.2 6.4 %copy-start.3 = (s32[1,128,256]{2,1,0:T(8,128)S(1)}, s32[1,128,256]{2,1,0:T(8,128)}, u32[]{:S(2)}) copy-start(s32[1,128,256]{2,1,0:T(8,128)} %param.14) | copy-start | bytes 393220
  2.2 6.4 %copy-start.4 = (s32[256]{0:T(256)S(1)}, s32[256]{0:T(256)}, u32[]{:S(2)}) copy-start(s32[256]{0:T(256)} %param.16) | copy-start | bytes 3076
  2.2 6.4 %copy-start.5 = (s32[256]{0:T(256)S(1)}, s32[256]{0:T(256)}, u32[]{:S(2)}) copy-start(s32[256]{0:T(256)} %param.15) | copy-start | bytes 3076
  2.3 18.5 %copy-start.1 = (f32[1,128,256]{2,1,0:T(8,128)S(1)}, f32[1,128,256]{2,1,0:T(8,128)}, u32[]{:S(2)}) copy-start(f32[1,128,256]{2,1,0:T(8,128)} %param.10) | copy-start | bytes 393220
  2.3 18.5 %copy-start.6 = (f32[1,128]{1,0:T(1,128)S(1)}, f32[1,128]{1,0:T(1,128)}, u32[]{:S(2)}) copy-start(f32[1,128]{1,0:T(1,128)} %param.17) | copy-start | bytes 1540
  2.4 14.2 %collective-permute-start = (f32[4,1,128,1]{3,2,1,0:T(8,128)S(1)}, f32[4,1,128,1]{3,2,1,0:T(8,128)S(1)}, u32[]{:S(2)}, u32[]{:S(2)}) collective-permute-start(f32[4,1,128,1]{3,2,1,0:T(8,128)S(1)} %get-tuple-element.34), channel_id=1, source_target_pairs={{0,4},{4,8},{8,12},{12,16},{16,20},{20,24},{24,28},{28,0},{1,5},{5... | collective-permute-start | bytes 6152 | tf_op jit(solution)/shard_map/ppermute | solution.py:19
  5.5 13.4 %collective-permute-start.1 = (f32[4,1,128,1]{3,2,1,0:T(8,128)S(1)}, f32[4,1,128,1]{3,2,1,0:T(8,128)S(1)}, u32[]{:S(2)}, u32[]{:S(2)}) collective-permute-start(f32[4,1,128,1]{3,2,1,0:T(8,128)S(1)} %get-tuple-element.35), channel_id=1, source_target_pairs={{4,0},{8,4},{12,8},{16,12},{20,16},{24,20},{28,24},{0,28},{5,1},{9... | collective-permute-start | bytes 6152 | tf_op jit(solution)/shard_map/ppermute | solution.py:21
  19.0 3.1 %collective-permute-start.2 = (f32[4,1,1,258]{3,2,1,0:T(1,128)S(1)}, f32[4,1,1,258]{3,2,1,0:T(1,128)S(1)}, u32[]{:S(2)}, u32[]{:S(2)}) collective-permute-start(f32[4,1,1,258]{3,2,1,0:T(1,128)S(1)} %get-tuple-element.24), channel_id=1, source_target_pairs={{0,1},{1,2},{2,3},{3,0},{4,5},{5,6},{6,7},{7,4},{8,9},{9,10},{10,1... | collective-permute-start | bytes 12392 | tf_op jit(solution)/shard_map/ppermute | solution.py:19
  19.0 3.1 %collective-permute-start.3 = (f32[4,1,1,258]{3,2,1,0:T(1,128)S(1)}, f32[4,1,1,258]{3,2,1,0:T(1,128)S(1)}, u32[]{:S(2)}, u32[]{:S(2)}) collective-permute-start(f32[4,1,1,258]{3,2,1,0:T(1,128)S(1)} %get-tuple-element.25), channel_id=1, source_target_pairs={{1,0},{2,1},{3,2},{0,3},{5,4},{6,5},{7,6},{4,7},{9,8},{10,9},{11,1... | collective-permute-start | bytes 12392 | tf_op jit(solution)/shard_map/ppermute | solution.py:21
  22.6 0.9 copy-start.2
  25.6 12.3 %collective-permute-start.4 = (f32[4,1,128,1]{3,2,1,0:T(8,128)}, f32[4,1,128,1]{3,2,1,0:T(8,128)S(1)}, u32[]{:S(2)}, u32[]{:S(2)}) collective-permute-start(f32[4,1,128,1]{3,2,1,0:T(8,128)} %get-tuple-element.33), channel_id=1, source_target_pairs={{0,4},{4,8},{8,12},{12,16},{16,20},{20,24},{24,28},{28,0},{1,5},{5... | collective-permute-start | bytes 6152 | tf_op jit(solution)/shard_map/ppermute | solution.py:19
  25.9 14.8 %collective-permute-start.5 = (f32[4,1,128,1]{3,2,1,0:T(8,128)}, f32[4,1,128,1]{3,2,1,0:T(8,128)S(1)}, u32[]{:S(2)}, u32[]{:S(2)}) collective-permute-start(f32[4,1,128,1]{3,2,1,0:T(8,128)} %get-tuple-element.32), channel_id=1, source_target_pairs={{4,0},{8,4},{12,8},{16,12},{20,16},{24,20},{28,24},{0,28},{5,1},{9... | collective-permute-start | bytes 6152 | tf_op jit(solution)/shard_map/ppermute | solution.py:21
  51.5 23.4 %collective-permute-start.6 = (f32[128,5,128]{2,1,0:T(8,128)S(1)}, f32[128,5,128]{2,1,0:T(8,128)S(1)}, u32[]{:S(2)}, u32[]{:S(2)}) collective-permute-start(f32[128,5,128]{2,1,0:T(8,128)S(1)} %get-tuple-element.23), channel_id=1, source_target_pairs={{0,4},{4,8},{8,12},{12,16},{16,20},{20,24},{24,28},{28,0},{1,5},{5... | collective-permute-start | bytes 983048 | tf_op jit(solution)/shard_map/ppermute | solution.py:19
  51.6 26.7 %collective-permute-start.7 = (f32[128,5,128]{2,1,0:T(8,128)S(1)}, f32[128,5,128]{2,1,0:T(8,128)S(1)}, u32[]{:S(2)}, u32[]{:S(2)}) collective-permute-start(f32[128,5,128]{2,1,0:T(8,128)S(1)} %get-tuple-element.22), channel_id=1, source_target_pairs={{4,0},{8,4},{12,8},{16,12},{20,16},{24,20},{28,24},{0,28},{5,1},{9... | collective-permute-start | bytes 983048 | tf_op jit(solution)/shard_map/ppermute | solution.py:21
  87.2 21.3 %collective-permute-start.8 = (f32[4,128]{0,1:T(8,128)S(1)}, f32[4,128]{0,1:T(8,128)S(1)}, u32[]{:S(2)}, u32[]{:S(2)}) collective-permute-start(f32[4,128]{0,1:T(8,128)S(1)} %slice_bitcast_fusion.4), channel_id=1, source_target_pairs={{0,4},{4,8},{8,12},{12,16},{16,20},{20,24},{24,28},{28,0},{1,5},{5... | collective-permute-start | bytes 6152 | tf_op jit(solution)/shard_map/ppermute | solution.py:31
where the time goes:
time: 116 us
  waiting for transfers between devices  42 us (36%)
  other arithmetic  37.8 us (33%)
  local copies, waits for them, and re-layouts  18 us (16%)
  starting transfers between devices  17.5 us (15%)
    ppermute x4, waiting for transfers between devices, padded_2(): lax.ppermute(tail, axis, [(i, (i + 1) % count) for i in range(count)])  33.7 us
    scatter-add x1, other arithmetic, on_device(): jax.ops.segment_sum(all_main, all_targets, num_segments=tile_count + 1)  17.3 us
    ppermute x4, starting transfers between devices, padded_2(): lax.ppermute(head, axis, [((i + 1) % count, i) for i in range(count)])  14 us
    ppermute x4, waiting for transfers between devices, padded_2(): lax.ppermute(head, axis, [((i + 1) % count, i) for i in range(count)])  8.3 us
    scatter x1, local copies, waits for them, and re-layouts, on_device(): jnp.zeros((2 * capacity + 1, 5, TILE), jnp.float32).at[slot_ids].set(packet)  7.22 us
    convert_element_type x1, other arithmetic, on_device(): incoming_labels.astype(jnp.int32)  4.99 us
    scatter-add x1, local copies, waits for them, and re-layouts, on_device(): result = gathered.at[:, :, 0].add(inside + entering)  4.26 us
    scatter-add x1, other arithmetic, on_device(): jax.ops.segment_sum(all_spill, edge_targets, num_segments=row_count + 1)  3.65 us
  transfers between devices with their start and end apart: 9, of which 7 were waited for; matrix products, arithmetic and copies ran while one was open for 20% of the time, Pallas kernels for 0%

commit v1 on v0

v1 whole, which is shorter than its diff:
```python
import functools

import jax
import jax.numpy as jnp
from jax import lax
from jax.experimental import pallas as pl
from jax.experimental.pallas import tpu as pltpu
from jax.sharding import PartitionSpec as P

TILE = 128
time_step = 0.05
EDGE = 8
RAW = 6


def near_pairs(count):
    return [(i, i ^ 1) for i in range(count)]


def far_pairs(count, wraps):
    pairs = []
    for i in range(1, count, 2):
        j = i + 1
        if j < count or wraps:
            pairs += [(i, j % count), (j % count, i)]
    return pairs


def acoustic(density, energy, material):
    first, second = material == 0, material == 1
    less_one = jnp.where(first, 0.4, jnp.where(second, 2.0 / 3.0, 2.0)).astype(jnp.float32)
    both = jnp.where(first, 1.4 * 0.4, jnp.where(second, 10.0 / 9.0, 6.0)).astype(jnp.float32)
    return density * jnp.sqrt(both * energy), less_one * density * energy


def column_sums(impedance, pressure, speed_x, speed_y, from_left):
    along_x, along_y = impedance * speed_x, impedance * speed_y
    up, down = along_y + pressure, along_y - pressure
    return (
        from_left(impedance) + impedance,
        from_left(along_x + pressure) + (along_x - pressure),
        from_left(up) + up,
        from_left(down) + down,
    )


def nodes(below, above):
    scale = 1.0 / (below[0] + above[0])
    return (below[1] + above[1]) * scale, (below[2] + above[3]) * scale


def cell_values(impedance, pressure, speed_x, speed_y, density, energy, lower, upper, from_right):
    side_x = lower[0] + upper[0]
    side_y = lower[1] + upper[1]
    rise_y = upper[1] - lower[1]
    square = lower[0] * lower[0] + upper[0] * upper[0] + lower[1] * lower[1] + upper[1] * upper[1]
    far_x = from_right(side_x)
    sum_x = side_x + far_x
    sum_y = side_y + from_right(side_y)
    half_z = (0.5 * time_step) * impedance
    volume = (far_x - side_x) + (rise_y + from_right(rise_y))
    relaxation = (square + from_right(square)) - speed_x * sum_x - speed_y * sum_y
    left = (0.5 * time_step) * side_x
    right = (0.5 * time_step) * far_x
    scale = 1.0 / (1.0 + (right - left))
    total = density * (energy + 0.5 * (speed_x * speed_x + speed_y * speed_y))
    values = (
        density * scale,
        (density * speed_x + half_z * (sum_x - 4.0 * speed_x)) * scale,
        (density * speed_y + half_z * (sum_y - 4.0 * speed_y)) * scale,
        (total + (half_z * relaxation - (0.5 * time_step) * pressure * volume)) * scale,
    )
    return values, left, right


def remap_weights(shift, left, right):
    start = shift + left
    stop = 1.0 + shift + right
    centre = 0.5 * (start + stop)
    low_own, high_own = jnp.maximum(start, 0.0), jnp.minimum(stop, 1.0)
    span_own = jnp.maximum(high_own - low_own, 0.0)
    low_next, high_next = jnp.maximum(start, 1.0), jnp.minimum(stop, 2.0)
    span_next = jnp.maximum(high_next - low_next, 0.0)
    return (
        span_own,
        span_own * (0.5 * (high_own + low_own) - centre),
        span_next,
        span_next * (0.5 * (high_next + low_next) - centre),
    )


def remapped_field(value, steepness, weights, from_left, from_right):
    back = value - from_left(value)
    fore = from_right(back)
    mean = 0.5 * (back + fore)
    rising = jnp.maximum(jnp.minimum(steepness * jnp.minimum(back, fore), mean), 0.0)
    falling = jnp.minimum(jnp.maximum(steepness * jnp.maximum(back, fore), mean), 0.0)
    slope = rising + falling
    own = weights[0] * value + weights[1] * slope
    return own + from_left(weights[2] * value + weights[3] * slope)


class Wide:
    def __init__(self, parts):
        self.parts = tuple(parts)

    def _with(self, other, op):
        if isinstance(other, Wide):
            return Wide(op(a, b) for a, b in zip(self.parts, other.parts))
        return Wide(op(a, other) for a in self.parts)

    def __add__(self, o):
        return self._with(o, lambda a, b: a + b)

    def __radd__(self, o):
        return self._with(o, lambda a, b: b + a)

    def __sub__(self, o):
        return self._with(o, lambda a, b: a - b)

    def __mul__(self, o):
        return self._with(o, lambda a, b: a * b)

    def __rmul__(self, o):
        return self._with(o, lambda a, b: b * a)


def wide_left(lane, parts):
    turned = [pltpu.roll(a, 1, 1) for a in parts]
    return [turned[0]] + [
        jnp.where(lane == 0, turned[i - 1], turned[i]) for i in range(1, len(turned))
    ]


def wide_right(lane, parts):
    width = parts[0].shape[-1]
    turned = [pltpu.roll(a, width - 1, 1) for a in parts]
    return [
        jnp.where(lane == width - 1, turned[i + 1], turned[i]) for i in range(len(turned) - 1)
    ] + [turned[-1]]


def halo_kernel(rho_lo, vel_lo, en_lo, mat_lo, rho_hi, vel_hi, en_hi, mat_hi, near_ref, far_ref):
    even = lax.axis_index("gy") % 2 == 0
    rows = rho_lo.shape[1]

    def stack(rho, vel, en, mat, row):
        pick = slice(row, row + 1)
        z, p = acoustic(rho[0, pick, :], en[0, pick, :], mat[0, pick, :])
        return [z, p, vel[0, 0, pick, :], vel[1, 0, pick, :]]

    bottom = stack(rho_lo, vel_lo, en_lo, mat_lo, 0)
    top = stack(rho_hi, vel_hi, en_hi, mat_hi, rows - 1)
    for k in range(4):
        near_ref[k : k + 1, :] = jnp.where(even, top[k], bottom[k])
        far_ref[k : k + 1, :] = jnp.where(even, bottom[k], top[k])


def block_kernel(
    rho_ref, vel_ref, en_ref, mat_ref, lim_ref, shift_ref, near_ref, far_ref,
    out_ref, first_ref, second_ref, edge_ref,
    sums_ref, node_ref, press_ref, shifts_ref, edges_ref, *, step,
):
    rows, cols = rho_ref.shape[1:]
    halves = range(cols // TILE)
    even_x = lax.axis_index("gx") % 2 == 0
    even_y = lax.axis_index("gy") % 2 == 0
    pad = 8

    def cut(array, h):
        return array[:, h * TILE : (h + 1) * TILE]

    near, far = near_ref[0:4, :], far_ref[0:4, :]
    below = jnp.where(even_y, far, near)
    above = jnp.where(even_y, near, far)
    lane1 = lax.broadcasted_iota(jnp.int32, (1, TILE), 1)
    for halo, at in ((below, pad - 1), (above, pad + rows)):
        parts = [[cut(halo[k : k + 1, :], h) for h in halves] for k in range(4)]
        left1 = lambda a: Wide(wide_left(lane1, a.parts))
        for s, total in enumerate(column_sums(*[Wide(q) for q in parts], left1)):
            for h in halves:
                sums_ref[s, h, at : at + 1, :] = total.parts[h]
    halo = jnp.concatenate([below, above], axis=0)
    lane8 = lax.broadcasted_iota(jnp.int32, (8, TILE), 1)
    corner = pltpu.roll(jnp.where(lane8 < TILE // 2, cut(halo, 0), cut(halo, len(halves) - 1)), EDGE, 1)
    corner = jnp.concatenate([corner, jnp.zeros((TILE - 8, TILE), jnp.float32)], axis=0)
    corner_t = corner.T[0 : 2 * EDGE, :]
    shifts_ref[...] = jnp.broadcast_to(shift_ref[...], (TILE, TILE)).T

    lane = lax.broadcasted_iota(jnp.int32, (step, TILE), 1)
    left = lambda a: Wide(wide_left(lane, a.parts))
    right = lambda a: Wide(wide_right(lane, a.parts))

    def at_rows(i, offset=0):
        return pl.ds(pl.multiple_of(i * step, step) + offset, step)

    def columns(h):
        return slice(h * TILE, (h + 1) * TILE)

    def first_pass(i, _):
        here = at_rows(i)
        rho = [rho_ref[0, here, columns(h)] for h in halves]
        en = [en_ref[0, here, columns(h)] for h in halves]
        mat = [mat_ref[0, here, columns(h)] for h in halves]
        sx = [vel_ref[0, 0, here, columns(h)] for h in halves]
        sy = [vel_ref[1, 0, here, columns(h)] for h in halves]
        both = [acoustic(rho[h], en[h], mat[h]) for h in halves]
        z, p = [b[0] for b in both], [b[1] for b in both]
        for h in halves:
            press_ref[0, h, here, :] = z[h]
            press_ref[1, h, here, :] = p[h]
        totals = column_sums(Wide(z), Wide(p), Wide(sx), Wide(sy), left)
        for s, total in enumerate(totals):
            for h in halves:
                sums_ref[s, h, at_rows(i, pad), :] = total.parts[h]
        lim = [lim_ref[0, here, columns(h)].astype(jnp.float32) for h in (0, len(halves) - 1)]
        mats = [mat[0].astype(jnp.float32), mat[-1].astype(jnp.float32)]
        edge = jnp.zeros((step, TILE), jnp.float32)
        ends = ((rho[0], rho[-1]), (sx[0], sx[-1]), (sy[0], sy[-1]), (en[0], en[-1]), mats, lim)
        for k, (start, stop) in enumerate(ends):
            turned = pltpu.roll(jnp.where(lane < TILE // 2, start, stop), (2 * k + 1) * EDGE, 1)
            edge = jnp.where(lane >= 2 * k * EDGE, turned, edge)
        edges_ref[here, :] = edge
        return 0

    lax.fori_loop(0, rows // step, first_pass, 0)

    def second_pass(i, _):
        for h in halves:
            under = [sums_ref[s, h, at_rows(i, pad - 1), :] for s in range(3)]
            over = [sums_ref[s, h, at_rows(i, pad), :] for s in (0, 1, 3)]
            nx, ny = nodes(under, [over[0], over[1], None, over[2]])
            node_ref[0, h, at_rows(i), :] = nx
            node_ref[1, h, at_rows(i), :] = ny
        return 0

    lax.fori_loop(0, rows // step, second_pass, 0)
    for h in halves:
        under = [sums_ref[s, h, rows + pad - 1 : rows + pad, :] for s in range(3)]
        over = [sums_ref[s, h, rows + pad : rows + pad + 1, :] for s in (0, 1, 3)]
        nx, ny = nodes(under, [over[0], over[1], None, over[2]])
        node_ref[0, h, rows : rows + 1, :] = nx
        node_ref[1, h, rows : rows + 1, :] = ny

    edge_t = edges_ref[...].T
    edge_ref[0 : 2 * RAW * EDGE, :] = edge_t[0 : 2 * RAW * EDGE, :]
    edge_ref[2 * RAW * EDGE :, :] = corner_t
    base = 4 * rows
    for k in range(RAW + 1):
        source = edge_t if k < RAW else corner_t
        at = 2 * k * EDGE if k < RAW else 0
        right_edge, left_edge = source[at : at + EDGE, :], source[at + EDGE : at + 2 * EDGE, :]
        spot = slice(base + k * EDGE, base + (k + 1) * EDGE)
        first_ref[spot, :] = jnp.where(even_x, right_edge, left_edge)
        second_ref[spot, :] = jnp.where(even_x, left_edge, right_edge)

    def third_pass(i, _):
        here = at_rows(i)
        wide = lambda ref, *at: Wide(ref[(*at, here, columns(h))] for h in halves)
        rho, en = wide(rho_ref, 0), wide(en_ref, 0)
        sx, sy = wide(vel_ref, 0, 0), wide(vel_ref, 1, 0)
        z = Wide(press_ref[0, h, here, :] for h in halves)
        p = Wide(press_ref[1, h, here, :] for h in halves)
        lower = [Wide(node_ref[d, h, here, :] for h in halves) for d in range(2)]
        upper = [Wide(node_ref[d, h, at_rows(i, 1), :] for h in halves) for d in range(2)]
        steepness = Wide(lim_ref[0, here, columns(h)].astype(jnp.float32) + 1.0 for h in halves)
        shift = shifts_ref[here, :]
        values, dl, dr = wide_cells(z, p, sx, sy, rho, en, lower, upper, right)
        weights = [remap_weights(shift, dl.parts[h], dr.parts[h]) for h in halves]
        weights = [Wide(w) for w in zip(*weights)]
        for f, value in enumerate(values):
            done = wide_field(value, steepness, weights, left, right)
            for h in halves:
                out_ref[f, here, columns(h)] = done.parts[h]
            ends = done.parts[0], done.parts[-1]
            spot = pl.ds(pl.multiple_of(f * rows + i * step, step), step)
            first_ref[spot, :] = jnp.where(even_x, ends[1], ends[0])
            second_ref[spot, :] = jnp.where(even_x, ends[0], ends[1])
        return 0

    lax.fori_loop(0, rows // step, third_pass, 0)


def wide_cells(z, p, sx, sy, rho, en, lower, upper, from_right):
    halves = range(len(z.parts))
    pieces = []
    for h in halves:
        lx, ly, ux, uy = (q.parts[h] for q in (*lower, *upper))
        pieces.append((lx + ux, ly + uy, uy - ly, lx * lx + ux * ux + ly * ly + uy * uy))
    far = [from_right(Wide(q)).parts for q in zip(*pieces)]
    results = []
    for h in halves:
        queue = [far[k][h] for k in (0, 1, 2, 3)]
        order = iter(queue)
        results.append(
            cell_values(
                z.parts[h], p.parts[h], sx.parts[h], sy.parts[h], rho.parts[h], en.parts[h],
                [q.parts[h] for q in lower], [q.parts[h] for q in upper], lambda _: next(order),
            )
        )
    values = [Wide(results[h][0][f] for h in halves) for f in range(4)]
    return values, Wide(r[1] for r in results), Wide(r[2] for r in results)


def wide_field(value, steepness, weights, left, right):
    back = value - left(value)
    fore = right(back)
    owns, nexts = [], []
    for h in range(len(value.parts)):
        b, f, k = back.parts[h], fore.parts[h], steepness.parts[h]
        mean = 0.5 * (b + f)
        rising = jnp.maximum(jnp.minimum(k * jnp.minimum(b, f), mean), 0.0)
        falling = jnp.minimum(jnp.maximum(k * jnp.maximum(b, f), mean), 0.0)
        slope = rising + falling
        w = [q.parts[h] for q in weights]
        owns.append(w[0] * value.parts[h] + w[1] * slope)
        nexts.append(w[2] * value.parts[h] + w[3] * slope)
    return Wide(owns) + left(Wide(nexts))


def merge_kernel(
    field_ref, edge_ref, first_ref, second_ref, shift_ref, owner_ref, out_ref, patch_ref, *, step
):
    rows, cols = field_ref.shape[1:]
    column, count = lax.axis_index("gx"), lax.axis_size("gx")
    even_x = column % 2 == 0
    base = 4 * rows
    span = 4 * EDGE

    def window(k):
        spot = slice(base + k * EDGE, base + (k + 1) * EDGE)
        from_near, from_far = first_ref[spot, :], second_ref[spot, :]
        return jnp.concatenate(
            [
                jnp.where(even_x, from_far, from_near),
                edge_ref[(2 * k + 1) * EDGE : (2 * k + 2) * EDGE, :],
                edge_ref[2 * k * EDGE : (2 * k + 1) * EDGE, :],
                jnp.where(even_x, from_near, from_far),
            ],
            axis=0,
        )

    left = lambda a: pltpu.roll(a, 1, 0)
    right = lambda a: pltpu.roll(a, span - 1, 0)
    rho, sx, sy, en, mat, lim = (window(k) for k in range(RAW))
    halo = window(RAW)
    z, p = acoustic(rho, en, mat)
    own = column_sums(z, p, sx, sy, left)
    spread = lambda k: jnp.broadcast_to(halo[:, k : k + 1], (span, rows))
    below = column_sums(*(spread(k) for k in range(4)), left)
    above = column_sums(*(spread(k) for k in range(4, 8)), left)
    lane = lax.broadcasted_iota(jnp.int32, (span, rows), 1)
    under = [jnp.where(lane == 0, b, pltpu.roll(a, 1, 1)) for a, b in zip(own, below)]
    over = [jnp.where(lane == rows - 1, b, pltpu.roll(a, rows - 1, 1)) for a, b in zip(own, above)]
    values, dl, dr = cell_values(
        z, p, sx, sy, rho, en, nodes(under, own), nodes(own, over), right
    )
    weights = remap_weights(shift_ref[...], dl, dr)
    fields = [remapped_field(v, lim + 1.0, weights, left, right) for v in values]
    patch_ref[...] = jnp.concatenate(fields, axis=0).T

    owner = owner_ref[...]
    def total(which):
        hits = jnp.where(owner == which, 1.0, 0.0)
        return jnp.sum(jnp.sum(hits, axis=1, keepdims=True), axis=0, keepdims=True)

    to_left = total((column + count - 1) % count)
    to_right = total((column + 1) % count)
    lane = lax.broadcasted_iota(jnp.int32, (step, TILE), 1)
    row_in = lax.broadcasted_iota(jnp.int32, (step, TILE), 0)
    head, tail = lane < 3, lane >= TILE - 2

    def one(i, _):
        here = pl.ds(pl.multiple_of(i * step, step), step)
        row = (row_in + i * step).astype(jnp.float32)
        goes_left, goes_right = row < to_left, row >= rows - to_right
        patch = patch_ref[here, :]
        for f in range(4):
            at_left = pltpu.roll(patch, (-(span * f + EDGE)) % TILE, 1)
            at_right = pltpu.roll(patch, (-(span * f + 3 * EDGE)) % TILE, 1)
            spot = pl.ds(pl.multiple_of(f * rows + i * step, step), step)
            from_near, from_far = first_ref[spot, :], second_ref[spot, :]
            own_0 = jnp.where(head, at_left, field_ref[f, here, 0:TILE])
            own_1 = jnp.where(tail, at_right, field_ref[f, here, TILE:])
            left_tile = jnp.where(tail, at_left, jnp.where(even_x, from_far, from_near))
            right_tile = jnp.where(head, at_right, jnp.where(even_x, from_near, from_far))
            out_ref[f, 0, here, 0:TILE] = jnp.where(
                goes_right, left_tile, jnp.where(goes_left, own_1, own_0)
            )
            out_ref[f, 0, here, TILE:] = jnp.where(
                goes_right, own_0, jnp.where(goes_left, right_tile, own_1)
            )
        return 0

    lax.fori_loop(0, rows // step, one, 0)


def on_device(density, velocity, energy, material, limiter, owners, dest_tile, tile_shift):
    planes, rows, cols = density.shape
    assert planes == 1 and rows == TILE and cols == 2 * TILE
    gx, gy = lax.axis_size("gx"), lax.axis_size("gy")
    f32 = jnp.float32
    vmem = pl.BlockSpec(memory_space=pltpu.VMEM)
    shape = jax.ShapeDtypeStruct

    low3 = pl.BlockSpec((1, 8, cols), lambda i: (0, 0, 0))
    low4 = pl.BlockSpec((2, 1, 8, cols), lambda i: (0, 0, 0, 0))
    last = rows // 8 - 1
    high3 = pl.BlockSpec((1, 8, cols), lambda i: (0, last, 0))
    high4 = pl.BlockSpec((2, 1, 8, cols), lambda i: (0, 0, last, 0))
    halo_spec = pl.BlockSpec((8, cols), lambda i: (0, 0))
    near, far = pl.pallas_call(
        halo_kernel,
        grid=(1,),
        in_specs=[low3, low4, low3, low3, high3, high4, high3, high3],
        out_specs=[halo_spec, halo_spec],
        out_shape=[shape((8, cols), f32)] * 2,
        name="halo",
    )(density, velocity, energy, material, density, velocity, energy, material)
    near = lax.ppermute(near, "gy", near_pairs(gy))
    far = lax.ppermute(far, "gy", far_pairs(gy, False))

    message = shape((4 * rows + (RAW + 1) * EDGE, TILE), f32)
    field, first, second, edge = pl.pallas_call(
        functools.partial(block_kernel, step=8),
        in_specs=[vmem] * 8,
        out_specs=[vmem] * 4,
        out_shape=[
            shape((4, rows, cols), f32),
            message,
            message,
            shape((2 * (RAW + 1) * EDGE, TILE), f32),
        ],
        scratch_shapes=[
            pltpu.VMEM((4, 2, rows + 16, TILE), f32),
            pltpu.VMEM((2, 2, rows + 8, TILE), f32),
            pltpu.VMEM((2, 2, rows, TILE), f32),
            pltpu.VMEM((TILE, TILE), f32),
            pltpu.VMEM((rows, TILE), f32),
        ],
        name="block",
    )(density, velocity, energy, material, limiter, tile_shift, near, far)
    first = lax.ppermute(first, "gx", near_pairs(gx))
    second = lax.ppermute(second, "gx", far_pairs(gx, True))

    return pl.pallas_call(
        functools.partial(merge_kernel, step=8),
        in_specs=[vmem] * 6,
        out_specs=vmem,
        out_shape=shape((4, planes, rows, cols), f32),
        scratch_shapes=[pltpu.VMEM((rows, TILE), f32)],
        name="merge",
    )(field, edge, first, second, tile_shift, owners.reshape(-1, TILE))


def solution(mesh):
    assert mesh.shape["gx"] % 2 == 0 and mesh.shape["gy"] % 2 == 0
    placed = (
        P(None, "gy", "gx"),
        P(None, None, "gy", "gx"),
        P(None, "gy", "gx"),
        P(None, "gy", "gx"),
        P(None, "gy", "gx"),
        P(("gx", "gy")),
        P(("gx", "gy")),
        P(None, "gy"),
    )
    return jax.shard_map(
        on_device, mesh=mesh, in_specs=placed, out_specs=P(None, None, "gy", "gx"), check_vma=False
    )
```

time: 116 us -> 34.2 us (0.29)
  the two profiles are of different devices: /device:TPU:0 before, /device:TPU:1 now
where the time goes in v1:
time: 34.2 us; the launch traced here: 34 us
  Pallas kernels  14.1 us (41%)
  starting transfers between devices  9.63 us (28%)
  waiting for transfers between devices  8.86 us (26%)
  local copies, waits for them, and re-layouts  1.41 us (4%)
    pallas_call x1, Pallas kernels, on_device(): pl.pallas_call(functools.partial(block_kernel, step=8), in_specs=[vmem] *...  9 us
    ppermute x1, waiting for transfers between devices, on_device(): first = lax.ppermute(first, 'gx', near_pairs(gx))  7.34 us
    ppermute x1, starting transfers between devices, on_device(): far = lax.ppermute(far, 'gy', far_pairs(gy, False))  4.47 us
    pallas_call x1, Pallas kernels, on_device(): pl.pallas_call(functools.partial(merge_kernel, step=8), in_specs=[vmem] *...  3.62 us
    ppermute x1, starting transfers between devices, on_device(): second = lax.ppermute(second, 'gx', far_pairs(gx, True))  3.26 us
    ppermute x1, starting transfers between devices, on_device(): first = lax.ppermute(first, 'gx', near_pairs(gx))  1.87 us
    ppermute x1, waiting for transfers between devices, on_device(): far = lax.ppermute(far, 'gy', far_pairs(gy, False))  1.51 us
    pallas_call x1, Pallas kernels, on_device(): pl.pallas_call(halo_kernel, grid=(1,), in_specs=[low3, low4, low3, low3,...  1.43 us
  transfers between devices with their start and end apart: 4, of which 2 were waited for; matrix products, arithmetic and copies ran while one was open for 0% of the time, Pallas kernels for 0%

profile of v1, /device:TPU:1, one launch (start us, length us, event | category | flops | bytes accessed | tf_op | source)
XLA Modules:
  0.0 34.0 jit_solution(10518002299759152830)
XLA Ops:
  0.0 1.4 %halo.1 = (f32[8,256]{1,0:T(8,128)}, f32[8,256]{1,0:T(8,128)}) custom-call(f32[1,128,256]{2,1,0:T(8,128)} %rho_ref.1, f32[2,1,128,256]{3,2,1,0:T(8,128)} %vel_ref.1, f32[1,128,256]{2,1,0:T(8,128)} %en_ref.1, s32[1,128,256]{2,1,0:T(8,128)} %mat_ref.1, f32[1,128,256]{2,1,0:T(8,128)} %rho_ref.1, f32[2,1,128,256]{3,2,1,0:T(8,128)} %vel_ref.1, ...), custom_call_target="tpu_custom_call" | custom-call | tf_op jit(solution)/shard_map/halo/pallas_call | solution.py:412
  1.4 0.0 collective-permute-start
  1.5 4.5 %collective-permute-start.1 = (f32[8,256]{1,0:T(8,128)}, f32[8,256]{1,0:T(8,128)S(1)}, u32[]{:S(2)}, u32[]{:S(2)}) collective-permute-start(f32[8,256]{1,0:T(8,128)} %get-tuple-element.12), channel_id=1, source_target_pairs={{1,2},{2,1},{5,6},{6,5},{9,10},{10,9},{13,14},{14,13},{17,18},{18,... | collective-permute-start | bytes 24584 | tf_op jit(solution)/shard_map/ppermute | solution.py:421
  5.9 0.0 collective-permute-done.near_ref
  5.9 0.0 copy-start.2
  6.0 1.5 %collective-permute-done.1.far_ref = f32[8,256]{1,0:T(8,128)S(1)} collective-permute-done((f32[8,256]{1,0:T(8,128)}, f32[8,256]{1,0:T(8,128)S(1)}, u32[]{:S(2)}, u32[]{:S(2)}) %collective-permute-start.1) | collective-permute-done | bytes 8224 | tf_op jit(solution)/shard_map/ppermute | solution.py:421
  7.5 0.0 copy-done.2
  7.5 0.0 copy-start.3
  7.5 0.6 %copy-done.3 = f32[8,256]{1,0:T(8,128)} copy-done((f32[8,256]{1,0:T(8,128)}, f32[8,256]{1,0:T(8,128)S(1)}, u32[]{:S(2)}) %copy-start.3) | copy-done | bytes 8216
  8.1 9.0 %block.1 = (f32[4,128,256]{2,1,0:T(8,128)}, f32[568,128]{1,0:T(8,128)}, f32[568,128]{1,0:T(8,128)}, f32[112,128]{1,0:T(8,128)}) custom-call(f32[1,128,256]{2,1,0:T(8,128)} %rho_ref.1, f32[2,1,128,256]{3,2,1,0:T(8,128)} %vel_ref.1, f32[1,128,256]{2,1,0:T(8,128)} %en_ref.1, s32[1,128,256]{2,1,0:T(8,128)} %mat_ref.1, s32[1,128,256]{2,1,0:T(8,128)} %lim_ref.1, ...), custom_call_target="tpu_custom_call" | custom-call | tf_op jit(solution)/shard_map/block/pallas_call | solution.py:424
  17.1 1.9 %collective-permute-start.2 = (f32[568,128]{1,0:T(8,128)}, f32[568,128]{1,0:T(8,128)S(1)}, u32[]{:S(2)}, u32[]{:S(2)}) collective-permute-start(f32[568,128]{1,0:T(8,128)} %get-tuple-element.15), channel_id=1, source_target_pairs={{0,4},{4,0},{8,12},{12,8},{16,20},{20,16},{24,28},{28,24},{1,5},{5... | collective-permute-start | bytes 872456 | tf_op jit(solution)/shard_map/ppermute | solution.py:443
  18.9 3.3 %collective-permute-start.3 = (f32[568,128]{1,0:T(8,128)}, f32[568,128]{1,0:T(8,128)S(1)}, u32[]{:S(2)}, u32[]{:S(2)}) collective-permute-start(f32[568,128]{1,0:T(8,128)} %get-tuple-element.16), channel_id=1, source_target_pairs={{4,8},{8,4},{12,16},{16,12},{20,24},{24,20},{28,0},{0,28},{5,9},{9... | collective-permute-start | bytes 872456 | tf_op jit(solution)/shard_map/ppermute | solution.py:444
  22.2 7.3 %collective-permute-done.2.first_ref = f32[568,128]{1,0:T(8,128)S(1)} collective-permute-done((f32[568,128]{1,0:T(8,128)}, f32[568,128]{1,0:T(8,128)S(1)}, u32[]{:S(2)}, u32[]{:S(2)}) %collective-permute-start.2) | collective-permute-done | bytes 290848 | tf_op jit(solution)/shard_map/ppermute | solution.py:443
  29.5 0.0 copy-start
  29.5 0.0 collective-permute-done.3.second_ref
  29.5 0.0 copy-start.1
  29.5 0.7 %copy-done = f32[568,128]{1,0:T(8,128)} copy-done((f32[568,128]{1,0:T(8,128)}, f32[568,128]{1,0:T(8,128)S(1)}, u32[]{:S(2)}) %copy-start) | copy-done | bytes 290840
  30.3 0.1 copy-done.1
  30.4 3.6 %merge.1 = f32[4,1,128,256]{3,2,1,0:T(8,128)} custom-call(f32[4,128,256]{2,1,0:T(8,128)} %get-tuple-element.13.field_ref, f32[112,128]{1,0:T(8,128)} %get-tuple-element.14.edge_ref, f32[568,128]{1,0:T(8,128)} %copy-done, f32[568,128]{1,0:T(8,128)} %copy-done.1, f32[1,128]{1,0:T(1,128)} %shift_ref.3, s32[2,128]{1,0:T(2,128)} %bitcast.1), custom_call_target="tpu_custom_call" | custom-call | tf_op jit(solution)/shard_map/merge/pallas_call | solution.py:446
Async XLA Ops:
  1.4 4.5 %collective-permute-start = (f32[8,256]{1,0:T(8,128)}, f32[8,256]{1,0:T(8,128)S(1)}, u32[]{:S(2)}, u32[]{:S(2)}) collective-permute-start(f32[8,256]{1,0:T(8,128)} %get-tuple-element.11), channel_id=1, source_target_pairs={{0,1},{1,0},{2,3},{3,2},{4,5},{5,4},{6,7},{7,6},{8,9},{9,8},{10,11... | collective-permute-start | bytes 24584 | tf_op jit(solution)/shard_map/ppermute | solution.py:420
  1.5 6.0 %collective-permute-start.1 = (f32[8,256]{1,0:T(8,128)}, f32[8,256]{1,0:T(8,128)S(1)}, u32[]{:S(2)}, u32[]{:S(2)}) collective-permute-start(f32[8,256]{1,0:T(8,128)} %get-tuple-element.12), channel_id=1, source_target_pairs={{1,2},{2,1},{5,6},{6,5},{9,10},{10,9},{13,14},{14,13},{17,18},{18,... | collective-permute-start | bytes 24584 | tf_op jit(solution)/shard_map/ppermute | solution.py:421
  5.9 1.5 %copy-start.2 = (f32[8,256]{1,0:T(8,128)}, f32[8,256]{1,0:T(8,128)S(1)}, u32[]{:S(2)}) copy-start(f32[8,256]{1,0:T(8,128)S(1)} %collective-permute-done.near_ref) | copy-start | bytes 24580
  7.5 0.6 %copy-start.3 = (f32[8,256]{1,0:T(8,128)}, f32[8,256]{1,0:T(8,128)S(1)}, u32[]{:S(2)}) copy-start(f32[8,256]{1,0:T(8,128)S(1)} %collective-permute-done.1.far_ref) | copy-start | bytes 24580
  17.1 12.5 %collective-permute-start.2 = (f32[568,128]{1,0:T(8,128)}, f32[568,128]{1,0:T(8,128)S(1)}, u32[]{:S(2)}, u32[]{:S(2)}) collective-permute-start(f32[568,128]{1,0:T(8,128)} %get-tuple-element.15), channel_id=1, source_target_pairs={{0,4},{4,0},{8,12},{12,8},{16,20},{20,16},{24,28},{28,24},{1,5},{5... | collective-permute-start | bytes 872456 | tf_op jit(solution)/shard_map/ppermute | solution.py:443
  18.9 10.6 %collective-permute-start.3 = (f32[568,128]{1,0:T(8,128)}, f32[568,128]{1,0:T(8,128)S(1)}, u32[]{:S(2)}, u32[]{:S(2)}) collective-permute-start(f32[568,128]{1,0:T(8,128)} %get-tuple-element.16), channel_id=1, source_target_pairs={{4,8},{8,4},{12,16},{16,12},{20,24},{24,20},{28,0},{0,28},{5,9},{9... | collective-permute-start | bytes 872456 | tf_op jit(solution)/shard_map/ppermute | solution.py:444
  29.5 0.7 %copy-start = (f32[568,128]{1,0:T(8,128)}, f32[568,128]{1,0:T(8,128)S(1)}, u32[]{:S(2)}) copy-start(f32[568,128]{1,0:T(8,128)S(1)} %collective-permute-done.2.first_ref) | copy-start | bytes 872452
  29.5 0.8 %copy-start.1 = (f32[568,128]{1,0:T(8,128)}, f32[568,128]{1,0:T(8,128)S(1)}, u32[]{:S(2)}) copy-start(f32[568,128]{1,0:T(8,128)S(1)} %collective-permute-done.3.second_ref) | copy-start | bytes 872452

commit v2 on v1

v2 whole, which is shorter than its diff:
```python
import functools

import jax
import jax.numpy as jnp
from jax import lax
from jax.experimental import pallas as pl
from jax.experimental.pallas import tpu as pltpu
from jax.sharding import PartitionSpec as P

TILE = 128
time_step = 0.05
STEP = 8
BLOCK = (4, 4, 4)
MERGE = 4
CHUNK = 32
VMEM_LIMIT = 8 << 20
EDGE = 8
RAW = 6


def near_pairs(count):
    return [(i, i ^ 1) for i in range(count)]


def far_pairs(count):
    pairs = []
    for i in range(1, count, 2):
        pairs += [(i, (i + 1) % count), ((i + 1) % count, i)]
    return pairs


def acoustic(density, energy, material):
    first, second = material == 0, material == 1
    less_one = jnp.where(first, 0.4, jnp.where(second, 2.0 / 3.0, 2.0)).astype(jnp.float32)
    both = jnp.where(first, 1.4 * 0.4, jnp.where(second, 10.0 / 9.0, 6.0)).astype(jnp.float32)
    return density * jnp.sqrt(both * energy), less_one * density * energy


def column_sums(impedance, pressure, speed_x, speed_y, from_left):
    along_x, along_y = impedance * speed_x, impedance * speed_y
    up, down = along_y + pressure, along_y - pressure
    return (
        from_left(impedance) + impedance,
        from_left(along_x + pressure) + (along_x - pressure),
        from_left(up) + up,
        from_left(down) + down,
    )


def nodes(below, above):
    scale = 1.0 / (below[0] + above[0])
    return (below[1] + above[1]) * scale, (below[2] + above[3]) * scale


def cell_values(impedance, pressure, speed_x, speed_y, density, energy, lower, upper, from_right):
    side_x = lower[0] + upper[0]
    side_y = lower[1] + upper[1]
    rise_y = upper[1] - lower[1]
    square = lower[0] * lower[0] + upper[0] * upper[0] + lower[1] * lower[1] + upper[1] * upper[1]
    far_x = from_right(side_x)
    sum_x = side_x + far_x
    sum_y = side_y + from_right(side_y)
    half_z = (0.5 * time_step) * impedance
    volume = (far_x - side_x) + (rise_y + from_right(rise_y))
    relaxation = (square + from_right(square)) - speed_x * sum_x - speed_y * sum_y
    left = (0.5 * time_step) * side_x
    right = (0.5 * time_step) * far_x
    scale = 1.0 / (1.0 + (right - left))
    total = density * (energy + 0.5 * (speed_x * speed_x + speed_y * speed_y))
    values = (
        density * scale,
        (density * speed_x + half_z * (sum_x - 4.0 * speed_x)) * scale,
        (density * speed_y + half_z * (sum_y - 4.0 * speed_y)) * scale,
        (total + (half_z * relaxation - (0.5 * time_step) * pressure * volume)) * scale,
    )
    return values, left, right


def remap_weights(shift, left, right):
    start = shift + left
    stop = 1.0 + shift + right
    centre = 0.5 * (start + stop)
    low_own, high_own = jnp.maximum(start, 0.0), jnp.minimum(stop, 1.0)
    span_own = jnp.maximum(high_own - low_own, 0.0)
    low_next, high_next = jnp.maximum(start, 1.0), jnp.minimum(stop, 2.0)
    span_next = jnp.maximum(high_next - low_next, 0.0)
    return (
        span_own,
        span_own * (0.5 * (high_own + low_own) - centre),
        span_next,
        span_next * (0.5 * (high_next + low_next) - centre),
    )


def remapped_field(value, steepness, weights, from_left, from_right):
    back = value - from_left(value)
    fore = from_right(back)
    mean = 0.5 * (back + fore)
    rising = jnp.maximum(jnp.minimum(steepness * jnp.minimum(back, fore), mean), 0.0)
    falling = jnp.minimum(jnp.maximum(steepness * jnp.maximum(back, fore), mean), 0.0)
    slope = rising + falling
    own = weights[0] * value + weights[1] * slope
    return own + from_left(weights[2] * value + weights[3] * slope)


class Wide:
    def __init__(self, parts):
        self.parts = tuple(parts)

    def _with(self, other, op):
        if isinstance(other, Wide):
            return Wide(op(a, b) for a, b in zip(self.parts, other.parts))
        return Wide(op(a, other) for a in self.parts)

    def __add__(self, o):
        return self._with(o, lambda a, b: a + b)

    def __radd__(self, o):
        return self._with(o, lambda a, b: b + a)

    def __sub__(self, o):
        return self._with(o, lambda a, b: a - b)

    def __mul__(self, o):
        return self._with(o, lambda a, b: a * b)

    def __rmul__(self, o):
        return self._with(o, lambda a, b: b * a)


def wide_left(lane, parts):
    turned = [pltpu.roll(a, 1, 1) for a in parts]
    return [turned[0]] + [
        jnp.where(lane == 0, turned[i - 1], turned[i]) for i in range(1, len(turned))
    ]


def wide_right(lane, parts):
    width = parts[0].shape[-1]
    turned = [pltpu.roll(a, width - 1, 1) for a in parts]
    return [
        jnp.where(lane == width - 1, turned[i + 1], turned[i]) for i in range(len(turned) - 1)
    ] + [turned[-1]]


def cut(array, h):
    return array[:, h * TILE : (h + 1) * TILE]


def lanes(h):
    return slice(h * TILE, (h + 1) * TILE)


def block_kernel(
    rho_hbm, vel_hbm, en_hbm, mat_hbm, lim_hbm, shift_hbm, owner_hbm,
    out_ref, first_ref, second_ref, edge_ref, rim_ref, near_ref, far_ref, row_ref,
    rho_ref, vel_ref, en_ref, mat_ref, lim_ref, shift_ref, owner_ref,
    sums_ref, node_ref, press_ref, shifts_ref, edges_ref, sems, small_sems,
):
    rows, cols = rho_ref.shape
    halves = range(cols // TILE)
    last = len(halves) - 1
    even_x = lax.axis_index("gx") % 2 == 0
    even_y = lax.axis_index("gy") % 2 == 0
    pad = 8
    chunks, inner = rows // CHUNK, CHUNK // STEP

    def copies(c):
        part = pl.ds(pl.multiple_of(c * CHUNK, CHUNK), CHUNK)
        return [
            pltpu.make_async_copy(rho_hbm.at[0, part, :], rho_ref.at[part, :], sems.at[0, c]),
            pltpu.make_async_copy(en_hbm.at[0, part, :], en_ref.at[part, :], sems.at[1, c]),
            pltpu.make_async_copy(mat_hbm.at[0, part, :], mat_ref.at[part, :], sems.at[2, c]),
            pltpu.make_async_copy(vel_hbm.at[:, 0, part, :], vel_ref.at[:, part, :], sems.at[3, c]),
            pltpu.make_async_copy(lim_hbm.at[0, part, :], lim_ref.at[part, :], sems.at[4, c]),
        ]

    for c in range(chunks):
        for copy in copies(c):
            copy.start()

    small = [
        pltpu.make_async_copy(shift_hbm, shift_ref, small_sems.at[0]),
        pltpu.make_async_copy(owner_hbm, owner_ref, small_sems.at[1]),
    ]
    for copy in small:
        copy.start()
    lane = lax.broadcasted_iota(jnp.int32, (STEP, TILE), 1)
    left = lambda a: Wide(wide_left(lane, a.parts))
    right = lambda a: Wide(wide_right(lane, a.parts))

    def at_rows(i, offset=0):
        return pl.ds(pl.multiple_of(i * STEP, STEP) + offset, STEP)

    def first_pass(i, _):
        here = at_rows(i)
        rho = [rho_ref[here, lanes(h)] for h in halves]
        en = [en_ref[here, lanes(h)] for h in halves]
        mat = [mat_ref[here, lanes(h)] for h in halves]
        sx = [vel_ref[0, here, lanes(h)] for h in halves]
        sy = [vel_ref[1, here, lanes(h)] for h in halves]
        both = [acoustic(rho[h], en[h], mat[h]) for h in halves]
        z, p = [b[0] for b in both], [b[1] for b in both]
        for h in halves:
            press_ref[0, h, here, :] = z[h]
            press_ref[1, h, here, :] = p[h]
        totals = column_sums(Wide(z), Wide(p), Wide(sx), Wide(sy), left)
        for s, total in enumerate(totals):
            for h in halves:
                sums_ref[s, h, at_rows(i, pad), :] = total.parts[h]
        lim = [lim_ref[here, lanes(h)].astype(jnp.float32) for h in (0, last)]
        mats = [mat[0].astype(jnp.float32), mat[-1].astype(jnp.float32)]
        edge = jnp.zeros((STEP, TILE), jnp.float32)
        ends = ((rho[0], rho[-1]), (sx[0], sx[-1]), (sy[0], sy[-1]), (en[0], en[-1]), mats, lim)
        for k, (start, stop) in enumerate(ends):
            turned = pltpu.roll(jnp.where(lane < TILE // 2, start, stop), (2 * k + 1) * EDGE, 1)
            edge = jnp.where(lane >= 2 * k * EDGE, turned, edge)
        edges_ref[here, :] = edge
        return 0

    def first_chunk(c, _):
        for copy in copies(c):
            copy.wait()
        step = lambda j, _: first_pass(c * inner + j, 0)
        return lax.fori_loop(0, inner, step, 0, unroll=BLOCK[0])

    for s in range(4):
        for h in halves:
            sums_ref[s, h, 0:pad, :] = jnp.full((pad, TILE), float(s == 0), jnp.float32)
            sums_ref[s, h, rows + pad :, :] = jnp.full((pad, TILE), float(s == 0), jnp.float32)
    lax.fori_loop(0, chunks, first_chunk, 0)

    def second_pass(i, _):
        for h in halves:
            under = [sums_ref[s, h, at_rows(i, pad - 1), :] for s in range(3)]
            over = [sums_ref[s, h, at_rows(i, pad), :] for s in (0, 1, 3)]
            nx, ny = nodes(under, [over[0], over[1], None, over[2]])
            node_ref[0, h, at_rows(i), :] = nx
            node_ref[1, h, at_rows(i), :] = ny
        return 0

    for copy in small:
        copy.wait()
    shifts_ref[...] = jnp.broadcast_to(shift_ref[...], (TILE, TILE)).T
    column, count = lax.axis_index("gx"), lax.axis_size("gx")
    owner = owner_ref[...]
    row_ref[0:1, :] = shift_ref[...]
    for k, which in enumerate(((column + count - 1) % count, (column + 1) % count)):
        hits = jnp.where(owner == which, 1.0, 0.0)
        total = jnp.sum(jnp.sum(hits, axis=1, keepdims=True), axis=0, keepdims=True)
        row_ref[k + 1 : k + 2, :] = jnp.broadcast_to(total, (1, TILE))
    lax.fori_loop(0, rows // STEP, second_pass, 0, unroll=BLOCK[1])
    for h in halves:
        for d in range(2):
            node_ref[d, h, rows : rows + STEP, :] = jnp.zeros((STEP, TILE), jnp.float32)

    for k in range(4):
        for h in halves:
            pick = lambda row: (
                press_ref[k, h, row : row + 1, :]
                if k < 2
                else vel_ref[k - 2, row : row + 1, lanes(h)]
            )
            top, bottom = pick(rows - 1), pick(0)
            near_ref[k : k + 1, lanes(h)] = jnp.where(even_y, top, bottom)
            far_ref[k : k + 1, lanes(h)] = jnp.where(even_y, bottom, top)
    for r, row in enumerate((0, rows - 1)):
        at, to = slice(row, row + 1), slice(r, r + 1)
        joint = slice(1, 2) if r == 0 else slice(rows - 1, rows)
        for h in halves:
            kept = [
                press_ref[0, h, at, :], press_ref[1, h, at, :],
                vel_ref[0, at, lanes(h)], vel_ref[1, at, lanes(h)],
                rho_ref[at, lanes(h)], en_ref[at, lanes(h)],
                lim_ref[at, lanes(h)].astype(jnp.float32), shifts_ref[at, :],
                *(sums_ref[s, h, pad + row : pad + row + 1, :] for s in range(4)),
                *(node_ref[d, h, joint, :] for d in range(2)),
            ]
            for k, value in enumerate(kept):
                rim_ref[k, to, lanes(h)] = value

    edge_ref[...] = edges_ref[...].T[0 : 2 * RAW * EDGE, :]

    def third_pass(i, _):
        here = at_rows(i)
        wide = lambda ref, *at: Wide(ref[(*at, here, lanes(h))] for h in halves)
        rho, en = wide(rho_ref), wide(en_ref)
        sx, sy = wide(vel_ref, 0), wide(vel_ref, 1)
        z = Wide(press_ref[0, h, here, :] for h in halves)
        p = Wide(press_ref[1, h, here, :] for h in halves)
        lower = [Wide(node_ref[d, h, here, :] for h in halves) for d in range(2)]
        upper = [Wide(node_ref[d, h, at_rows(i, 1), :] for h in halves) for d in range(2)]
        steepness = Wide(lim_ref[here, lanes(h)].astype(jnp.float32) + 1.0 for h in halves)
        shift = shifts_ref[here, :]
        values, dl, dr = wide_cells(z, p, sx, sy, rho, en, lower, upper, right)
        weights = [remap_weights(shift, dl.parts[h], dr.parts[h]) for h in halves]
        weights = [Wide(w) for w in zip(*weights)]
        for f, value in enumerate(values):
            done = wide_field(value, steepness, weights, left, right)
            for h in halves:
                out_ref[f, here, lanes(h)] = done.parts[h]
            ends = done.parts[0], done.parts[-1]
            spot = pl.ds(pl.multiple_of(f * rows + i * STEP, STEP), STEP)
            first_ref[spot, :] = jnp.where(even_x, ends[1], ends[0])
            second_ref[spot, :] = jnp.where(even_x, ends[0], ends[1])
        return 0

    lax.fori_loop(0, rows // STEP, third_pass, 0, unroll=BLOCK[2])


def rim_kernel(near_ref, far_ref, kept_ref, edge_ref, rows_ref, first_ref, second_ref, corner_ref):
    cols = near_ref.shape[-1]
    halves = range(cols // TILE)
    even_x = lax.axis_index("gx") % 2 == 0
    level, levels = lax.axis_index("gy"), lax.axis_size("gy")
    even_y = level % 2 == 0
    near, far = near_ref[0:4, :], far_ref[0:4, :]
    below = jnp.where(level == 0, 0.0, jnp.where(even_y, far, near))
    above = jnp.where(level == levels - 1, 0.0, jnp.where(even_y, near, far))

    lane = lax.broadcasted_iota(jnp.int32, (8, TILE), 1)
    bottom = lax.broadcasted_iota(jnp.int32, (8, TILE), 0) == 0
    left = lambda a: Wide(wide_left(lane, a.parts))
    right = lambda a: Wide(wide_right(lane, a.parts))

    kept = [Wide(kept_ref[k, :, lanes(h)] for h in halves) for k in range(14)]
    z, p, sx, sy, rho, en, lim, shift = kept[:8]
    own, joint = kept[8:12], kept[12:14]
    outer = [
        Wide(jnp.where(bottom, cut(below[k : k + 1, :], h), cut(above[k : k + 1, :], h)) for h in halves)
        for k in range(4)
    ]
    outer = column_sums(*outer, left)
    under, over = [], []
    for a, b in zip(outer, own):
        under.append(Wide(jnp.where(bottom, x, y) for x, y in zip(a.parts, b.parts)))
        over.append(Wide(jnp.where(bottom, y, x) for x, y in zip(a.parts, b.parts)))
    fresh = [nodes([q.parts[h] for q in under], [q.parts[h] for q in over]) for h in halves]
    fresh = [Wide(q) for q in zip(*fresh)]
    lower = [Wide(jnp.where(bottom, x, y) for x, y in zip(a.parts, b.parts)) for a, b in zip(fresh, joint)]
    upper = [Wide(jnp.where(bottom, y, x) for x, y in zip(a.parts, b.parts)) for a, b in zip(fresh, joint)]
    values, dl, dr = wide_cells(z, p, sx, sy, rho, en, lower, upper, right)
    weights = [remap_weights(shift.parts[h], dl.parts[h], dr.parts[h]) for h in halves]
    weights = [Wide(w) for w in zip(*weights)]
    steepness = Wide(q + 1.0 for q in lim.parts)
    for f, value in enumerate(values):
        done = wide_field(value, steepness, weights, left, right)
        for h in halves:
            rows_ref[2 * f : 2 * f + 2, lanes(h)] = done.parts[h][0:2, :]
        ends = done.parts[0][0:2, :], done.parts[-1][0:2, :]
        first_ref[2 * f : 2 * f + 2, :] = jnp.where(even_x, ends[1], ends[0])
        second_ref[2 * f : 2 * f + 2, :] = jnp.where(even_x, ends[0], ends[1])

    halo = jnp.concatenate([below, above], axis=0)
    corner = pltpu.roll(jnp.where(lane < TILE // 2, cut(halo, 0), cut(halo, len(halves) - 1)), EDGE, 1)
    corner = jnp.concatenate([corner, jnp.zeros((TILE - 8, TILE), jnp.float32)], axis=0)
    corner_t = corner.T[0 : 2 * EDGE, :]
    corner_ref[...] = corner_t
    for k in range(RAW + 1):
        at = 2 * k * EDGE
        if k < RAW:
            right_edge, left_edge = edge_ref[at : at + EDGE, :], edge_ref[at + EDGE : at + 2 * EDGE, :]
        else:
            right_edge, left_edge = corner_t[0:EDGE, :], corner_t[EDGE:, :]
        spot = slice(8 + k * EDGE, 8 + (k + 1) * EDGE)
        first_ref[spot, :] = jnp.where(even_x, right_edge, left_edge)
        second_ref[spot, :] = jnp.where(even_x, left_edge, right_edge)


def edge_kernel(edge_ref, corner_ref, first_ref, second_ref, row_ref, patch_ref):
    rows = patch_ref.shape[0]
    even_x = lax.axis_index("gx") % 2 == 0
    span = 4 * EDGE

    def window(k):
        spot = slice(8 + k * EDGE, 8 + (k + 1) * EDGE)
        from_near, from_far = first_ref[spot, :], second_ref[spot, :]
        own, at = (edge_ref, 2 * k * EDGE) if k < RAW else (corner_ref, 0)
        return jnp.concatenate(
            [
                jnp.where(even_x, from_far, from_near),
                own[at + EDGE : at + 2 * EDGE, :],
                own[at : at + EDGE, :],
                jnp.where(even_x, from_near, from_far),
            ],
            axis=0,
        )

    left = lambda a: pltpu.roll(a, 1, 0)
    right = lambda a: pltpu.roll(a, span - 1, 0)
    rho, sx, sy, en, mat, lim = (window(k) for k in range(RAW))
    halo = window(RAW)
    z, p = acoustic(rho, en, mat)
    own = column_sums(z, p, sx, sy, left)
    spread = lambda k: jnp.broadcast_to(halo[:, k : k + 1], (span, rows))
    below = column_sums(*(spread(k) for k in range(4)), left)
    above = column_sums(*(spread(k) for k in range(4, 8)), left)
    lane = lax.broadcasted_iota(jnp.int32, (span, rows), 1)
    under = [jnp.where(lane == 0, b, pltpu.roll(a, 1, 1)) for a, b in zip(own, below)]
    over = [jnp.where(lane == rows - 1, b, pltpu.roll(a, rows - 1, 1)) for a, b in zip(own, above)]
    values, dl, dr = cell_values(
        z, p, sx, sy, rho, en, nodes(under, own), nodes(own, over), right
    )
    weights = remap_weights(row_ref[0:1, :], dl, dr)
    fields = [remapped_field(v, lim + 1.0, weights, left, right) for v in values]
    patch_ref[...] = jnp.concatenate(fields, axis=0).T


def merge_kernel(
    field_ref, rows_ref, first_ref, second_ref, small_first_ref, small_second_ref, patch_ref,
    row_ref, out_hbm, out_ref, sems,
):
    rows = field_ref.shape[1]
    even_x = lax.axis_index("gx") % 2 == 0
    span = 4 * EDGE
    chunks, inner = rows // CHUNK, CHUNK // STEP

    to_left, to_right = row_ref[1:2, :], row_ref[2:3, :]

    def put(here, row, patch, pick_own, pick_sent):
        goes_left, goes_right = row < to_left, row >= rows - to_right
        lane = lax.broadcasted_iota(jnp.int32, patch.shape, 1)
        head, tail = lane < 3, lane >= TILE - 2
        for f in range(4):
            at_left = pltpu.roll(patch, (-(span * f + EDGE)) % TILE, 1)
            at_right = pltpu.roll(patch, (-(span * f + 3 * EDGE)) % TILE, 1)
            from_near, from_far = pick_sent(f)
            own_0 = jnp.where(head, at_left, pick_own(f, 0))
            own_1 = jnp.where(tail, at_right, pick_own(f, 1))
            left_tile = jnp.where(tail, at_left, jnp.where(even_x, from_far, from_near))
            right_tile = jnp.where(head, at_right, jnp.where(even_x, from_near, from_far))
            out_ref[f, here, lanes(0)] = jnp.where(
                goes_right, left_tile, jnp.where(goes_left, own_1, own_0)
            )
            out_ref[f, here, lanes(1)] = jnp.where(
                goes_right, own_0, jnp.where(goes_left, right_tile, own_1)
            )

    row_in = lax.broadcasted_iota(jnp.int32, (STEP, TILE), 0)

    def one(i, _):
        here = pl.ds(pl.multiple_of(i * STEP, STEP), STEP)

        def sent(f):
            spot = pl.ds(pl.multiple_of(f * rows + i * STEP, STEP), STEP)
            return first_ref[spot, :], second_ref[spot, :]

        row = (row_in + i * STEP).astype(jnp.float32)
        put(here, row, patch_ref[here, :], lambda f, h: field_ref[f, here, lanes(h)], sent)
        return 0

    def rim(r):
        row = r * (rows - 1)
        here = slice(row, row + 1)

        def sent(f):
            spot = slice(2 * f + r, 2 * f + r + 1)
            return small_first_ref[spot, :], small_second_ref[spot, :]

        own = lambda f, h: rows_ref[2 * f + r : 2 * f + r + 1, lanes(h)]
        put(here, jnp.full((1, TILE), float(row)), patch_ref[here, :], own, sent)

    def copy(c):
        part = pl.ds(pl.multiple_of(c * CHUNK, CHUNK), CHUNK)
        return pltpu.make_async_copy(out_ref.at[:, part, :], out_hbm.at[:, 0, part, :], sems.at[c])

    def chunk(c, _):
        lax.fori_loop(0, inner, lambda j, _: one(c * inner + j, 0), 0, unroll=MERGE)
        pl.when(c == 0)(lambda: rim(0))
        pl.when(c == chunks - 1)(lambda: rim(1))
        copy(c).start()
        return 0

    lax.fori_loop(0, chunks, chunk, 0)
    for c in range(chunks):
        copy(c).wait()


def on_device(density, velocity, energy, material, limiter, owners, dest_tile, tile_shift):
    planes, rows, cols = density.shape
    assert planes == 1 and rows == TILE and cols == 2 * TILE
    gx, gy = lax.axis_size("gx"), lax.axis_size("gy")
    f32 = jnp.float32
    vmem = pl.BlockSpec(memory_space=pltpu.VMEM)
    hbm = pl.BlockSpec(memory_space=pltpu.HBM)
    shape = lambda *dims: jax.ShapeDtypeStruct(dims, f32)
    params = pltpu.CompilerParams(vmem_limit_bytes=VMEM_LIMIT)
    chunks = rows // CHUNK
    stay = lambda array: pltpu.with_memory_space_constraint(array, pltpu.HBM)

    field, first, second, edge, kept, near, far, per_row = pl.pallas_call(
        block_kernel,
        in_specs=[hbm] * 7,
        out_specs=[vmem] * 8,
        out_shape=[
            shape(4, rows, cols),
            shape(4 * rows, TILE),
            shape(4 * rows, TILE),
            shape(2 * RAW * EDGE, TILE),
            shape(14, 8, cols),
            shape(8, cols),
            shape(8, cols),
            shape(8, TILE),
        ],
        scratch_shapes=[
            pltpu.VMEM((rows, cols), f32),
            pltpu.VMEM((2, rows, cols), f32),
            pltpu.VMEM((rows, cols), f32),
            pltpu.VMEM((rows, cols), jnp.int32),
            pltpu.VMEM((rows, cols), jnp.int32),
            pltpu.VMEM((1, rows), f32),
            pltpu.VMEM((rows * cols // TILE // TILE, TILE), jnp.int32),
            pltpu.VMEM((4, 2, rows + 16, TILE), f32),
            pltpu.VMEM((2, 2, rows + 8, TILE), f32),
            pltpu.VMEM((2, 2, rows, TILE), f32),
            pltpu.VMEM((TILE, TILE), f32),
            pltpu.VMEM((rows, TILE), f32),
            pltpu.SemaphoreType.DMA((5, chunks)),
            pltpu.SemaphoreType.DMA((2,)),
        ],
        compiler_params=params,
        name="block",
    )(*map(stay, (density, velocity, energy, material, limiter, tile_shift, owners.reshape(-1, TILE))))
    first = lax.ppermute(first, "gx", near_pairs(gx))
    near = lax.ppermute(near, "gy", near_pairs(gy))
    far = lax.ppermute(far, "gy", far_pairs(gy))
    second = lax.ppermute(second, "gx", far_pairs(gx))

    small = shape(8 + (RAW + 1) * EDGE, TILE)
    outer_rows, small_first, small_second, corner = pl.pallas_call(
        rim_kernel,
        in_specs=[vmem] * 4,
        out_specs=[vmem] * 4,
        out_shape=[shape(8, cols), small, small, shape(2 * EDGE, TILE)],
        compiler_params=params,
        name="rim",
    )(near, far, kept, edge)
    small_first = lax.ppermute(small_first, "gx", near_pairs(gx))
    small_second = lax.ppermute(small_second, "gx", far_pairs(gx))

    patch = pl.pallas_call(
        edge_kernel,
        in_specs=[vmem] * 5,
        out_specs=vmem,
        out_shape=shape(rows, TILE),
        compiler_params=params,
        name="edge",
    )(edge, corner, small_first, small_second, per_row)

    return pl.pallas_call(
        merge_kernel,
        in_specs=[vmem] * 8,
        out_specs=hbm,
        out_shape=shape(4, planes, rows, cols),
        scratch_shapes=[pltpu.VMEM((4, rows, cols), f32), pltpu.SemaphoreType.DMA((chunks,))],
        compiler_params=params,
        name="merge",
    )(
        field, outer_rows, first, second, small_first, small_second, patch, per_row,
    )


def wide_cells(z, p, sx, sy, rho, en, lower, upper, from_right):
    halves = range(len(z.parts))
    pieces = []
    for h in halves:
        lx, ly, ux, uy = (q.parts[h] for q in (*lower, *upper))
        pieces.append((lx + ux, ly + uy, uy - ly, lx * lx + ux * ux + ly * ly + uy * uy))
    far = [from_right(Wide(q)).parts for q in zip(*pieces)]
    results = []
    for h in halves:
        queue = [far[k][h] for k in (0, 1, 2, 3)]
        order = iter(queue)
        results.append(
            cell_values(
                z.parts[h], p.parts[h], sx.parts[h], sy.parts[h], rho.parts[h], en.parts[h],
                [q.parts[h] for q in lower], [q.parts[h] for q in upper], lambda _: next(order),
            )
        )
    values = [Wide(results[h][0][f] for h in halves) for f in range(4)]
    return values, Wide(r[1] for r in results), Wide(r[2] for r in results)


def wide_field(value, steepness, weights, left, right):
    back = value - left(value)
    fore = right(back)
    owns, nexts = [], []
    for h in range(len(value.parts)):
        b, f, k = back.parts[h], fore.parts[h], steepness.parts[h]
        mean = 0.5 * (b + f)
        rising = jnp.maximum(jnp.minimum(k * jnp.minimum(b, f), mean), 0.0)
        falling = jnp.minimum(jnp.maximum(k * jnp.maximum(b, f), mean), 0.0)
        slope = rising + falling
        w = [q.parts[h] for q in weights]
        owns.append(w[0] * value.parts[h] + w[1] * slope)
        nexts.append(w[2] * value.parts[h] + w[3] * slope)
    return Wide(owns) + left(Wide(nexts))


def solution(mesh):
    assert mesh.shape["gx"] % 2 == 0 and mesh.shape["gy"] % 2 == 0
    placed = (
        P(None, "gy", "gx"),
        P(None, None, "gy", "gx"),
        P(None, "gy", "gx"),
        P(None, "gy", "gx"),
        P(None, "gy", "gx"),
        P(("gx", "gy")),
        P(("gx", "gy")),
        P(None, "gy"),
    )
    return jax.shard_map(
        on_device, mesh=mesh, in_specs=placed, out_specs=P(None, None, "gy", "gx"), check_vma=False
    )
```

time: 34.2 us -> 22.2 us (0.65)
  the two profiles are of different devices: /device:TPU:1 before, /device:TPU:0 now
where the time goes in v2:
time: 22.2 us; the launch traced here: 22.1 us
  starting transfers between devices  10.2 us (46%)
  waiting for transfers between devices  6.44 us (29%)
  Pallas kernels  5.41 us (24%)
    ppermute x1, waiting for transfers between devices, on_device(): small_first = lax.ppermute(small_first, 'gx', near_pairs(gx))  3.62 us
    ppermute x1, starting transfers between devices, on_device(): second = lax.ppermute(second, 'gx', far_pairs(gx))  3.54 us
    pallas_call x1, Pallas kernels, on_device(): pl.pallas_call(block_kernel, in_specs=[hbm] * 7, out_specs=[vmem] * 8, ou...  3.41 us
    ppermute x1, starting transfers between devices, on_device(): first = lax.ppermute(first, 'gx', near_pairs(gx))  3.06 us
    ppermute x1, starting transfers between devices, on_device(): small_second = lax.ppermute(small_second, 'gx', far_pairs(gx))  1.9 us
    ppermute x1, starting transfers between devices, on_device(): far = lax.ppermute(far, 'gy', far_pairs(gy))  1.6 us
    ppermute x1, waiting for transfers between devices, on_device(): far = lax.ppermute(far, 'gy', far_pairs(gy))  1.47 us
    ppermute x1, waiting for transfers between devices, on_device(): small_second = lax.ppermute(small_second, 'gx', far_pairs(gx))  1.34 us
  transfers between devices with their start and end apart: 6, of which 3 were waited for; matrix products, arithmetic and copies ran while one was open for 0% of the time, Pallas kernels for 3%

profile of v2, /device:TPU:0, one launch (start us, length us, event | category | flops | bytes accessed | tf_op | source)
XLA Modules:
  0.0 22.1 jit_solution(10214453037275113460)
XLA Ops:
  0.0 3.4 %block.1 = (f32[4,128,256]{2,1,0:T(8,128)S(1)}, f32[512,128]{1,0:T(8,128)S(1)}, f32[512,128]{1,0:T(8,128)S(1)}, f32[96,128]{1,0:T(8,128)S(1)}, f32[14,8,256]{2,1...) custom-call(f32[1,128,256]{2,1,0:T(8,128)} %rho_hbm.1, ...), custom_call_target="tpu_custom_call" | custom-call | tf_op jit(solution)/shard_map/block/pallas_call | solution.py:491
  3.4 3.1 %collective-permute-start.2 = (f32[512,128]{1,0:T(8,128)S(1)}, f32[512,128]{1,0:T(8,128)S(1)}, u32[]{:S(2)}, u32[]{:S(2)}) collective-permute-start(f32[512,128]{1,0:T(8,128)S(1)} %get-tuple-element.23), channel_id=1, source_target_pairs={{0,4},{4,0},{8,12},{12,8},{16,20},{20,16},{24,28},{28,24},{1,5},{5... | collective-permute-start | bytes 786440 | tf_op jit(solution)/shard_map/ppermute | solution.py:524
  6.5 3.5 %collective-permute-start.3 = (f32[512,128]{1,0:T(8,128)S(1)}, f32[512,128]{1,0:T(8,128)S(1)}, u32[]{:S(2)}, u32[]{:S(2)}) collective-permute-start(f32[512,128]{1,0:T(8,128)S(1)} %get-tuple-element.24), channel_id=1, source_target_pairs={{4,8},{8,4},{12,16},{16,12},{20,24},{24,20},{28,0},{0,28},{5,9},{9... | collective-permute-start | bytes 786440 | tf_op jit(solution)/shard_map/ppermute | solution.py:527
  10.0 0.0 collective-permute-start
  10.0 1.6 %collective-permute-start.1 = (f32[8,256]{1,0:T(8,128)S(1)}, f32[8,256]{1,0:T(8,128)S(1)}, u32[]{:S(2)}, u32[]{:S(2)}) collective-permute-start(f32[8,256]{1,0:T(8,128)S(1)} %get-tuple-element.19), channel_id=1, source_target_pairs={{1,2},{2,1},{3,0},{0,3},{5,6},{6,5},{7,4},{4,7},{9,10},{10,9},{11,... | collective-permute-start | bytes 24584 | tf_op jit(solution)/shard_map/ppermute | solution.py:526
  11.6 0.0 collective-permute-done.near_ref
  11.6 1.5 %collective-permute-done.1.far_ref = f32[8,256]{1,0:T(8,128)S(1)} collective-permute-done((f32[8,256]{1,0:T(8,128)S(1)}, f32[8,256]{1,0:T(8,128)S(1)}, u32[]{:S(2)}, u32[]{:S(2)}) %collective-permute-start.1) | collective-permute-done | bytes 8224 | tf_op jit(solution)/shard_map/ppermute | solution.py:526
  13.1 0.4 %rim.1 = (f32[8,256]{1,0:T(8,128)S(1)}, f32[64,128]{1,0:T(8,128)S(1)}, f32[64,128]{1,0:T(8,128)S(1)}, f32[16,128]{1,0:T(8,128)S(1)}) custom-call(f32[8,256]{1,0:T(8,128)S(1)} %collective-permute-done.near_ref, f32[8,256]{1,0:T(8,128)S(1)} %collective-permute-done.1.far_ref, f32[14,8,256]{2,1,0:T(8,128)S(1)} %get-tuple-element.20.kept_ref, ...), custom_call_target="tpu_custom_call" | custom-call | tf_op jit(solution)/shard_map/rim/pallas_call | solution.py:530
  13.5 0.1 collective-permute-start.4
  13.6 1.9 %collective-permute-start.5 = (f32[64,128]{1,0:T(8,128)S(1)}, f32[64,128]{1,0:T(8,128)S(1)}, u32[]{:S(2)}, u32[]{:S(2)}) collective-permute-start(f32[64,128]{1,0:T(8,128)S(1)} %get-tuple-element.26), channel_id=1, source_target_pairs={{4,8},{8,4},{12,16},{16,12},{20,24},{24,20},{28,0},{0,28},{5,9},{9... | collective-permute-start | bytes 98312 | tf_op jit(solution)/shard_map/ppermute | solution.py:539
  15.5 3.6 %collective-permute-done.4.first_ref.small_first_ref = f32[64,128]{1,0:T(8,128)S(1)} collective-permute-done((f32[64,128]{1,0:T(8,128)S(1)}, f32[64,128]{1,0:T(8,128)S(1)}, u32[]{:S(2)}, u32[]{:S(2)}) %collective-permute-start.4) | collective-permute-done | bytes 32800 | tf_op jit(solution)/shard_map/ppermute | solution.py:538
  19.1 1.3 %collective-permute-done.5.second_ref.small_second_ref = f32[64,128]{1,0:T(8,128)S(1)} collective-permute-done((f32[64,128]{1,0:T(8,128)S(1)}, f32[64,128]{1,0:T(8,128)S(1)}, u32[]{:S(2)}, u32[]{:S(2)}) %collective-permute-start.5) | collective-permute-done | bytes 32800 | tf_op jit(solution)/shard_map/ppermute | solution.py:539
  20.4 0.3 %edge.1.patch_ref = f32[128,128]{1,0:T(8,128)S(1)} custom-call(f32[96,128]{1,0:T(8,128)S(1)} %get-tuple-element.21.edge_ref, f32[16,128]{1,0:T(8,128)S(1)} %get-tuple-element.27.corner_ref, f32[64,128]{1,0:T(8,128)S(1)} %collective-permute-done.4.first_ref.small_first_ref, f32[64,128]{1,0:T(8,128)S(1)} %collective-permute-done.5.second_ref.small_second_ref, ...), custom_call_target="tpu_custom_call" | custom-call | tf_op jit(solution)/shard_map/edge/pallas_call | solution.py:541
  20.7 0.0 collective-permute-done.2.first_ref
  20.8 0.0 collective-permute-done.3.second_ref
  20.8 1.3 %merge.1 = f32[4,1,128,256]{3,2,1,0:T(8,128)} custom-call(f32[4,128,256]{2,1,0:T(8,128)S(1)} %get-tuple-element.17.field_ref, f32[8,256]{1,0:T(8,128)S(1)} %get-tuple-element.22.rows_ref, f32[512,128]{1,0:T(8,128)S(1)} %collective-permute-done.2.first_ref, f32[512,128]{1,0:T(8,128)S(1)} %collective-permute-done.3.second_ref, ...), custom_call_target="tpu_custom_call" | custom-call | tf_op jit(solution)/shard_map/merge/pallas_call | solution.py:550
Async XLA Ops:
  3.4 17.3 %collective-permute-start.2 = (f32[512,128]{1,0:T(8,128)S(1)}, f32[512,128]{1,0:T(8,128)S(1)}, u32[]{:S(2)}, u32[]{:S(2)}) collective-permute-start(f32[512,128]{1,0:T(8,128)S(1)} %get-tuple-element.23), channel_id=1, source_target_pairs={{0,4},{4,0},{8,12},{12,8},{16,20},{20,16},{24,28},{28,24},{1,5},{5... | collective-permute-start | bytes 786440 | tf_op jit(solution)/shard_map/ppermute | solution.py:524
  6.5 14.3 %collective-permute-start.3 = (f32[512,128]{1,0:T(8,128)S(1)}, f32[512,128]{1,0:T(8,128)S(1)}, u32[]{:S(2)}, u32[]{:S(2)}) collective-permute-start(f32[512,128]{1,0:T(8,128)S(1)} %get-tuple-element.24), channel_id=1, source_target_pairs={{4,8},{8,4},{12,16},{16,12},{20,24},{24,20},{28,0},{0,28},{5,9},{9... | collective-permute-start | bytes 786440 | tf_op jit(solution)/shard_map/ppermute | solution.py:527
  10.0 1.6 %collective-permute-start = (f32[8,256]{1,0:T(8,128)S(1)}, f32[8,256]{1,0:T(8,128)S(1)}, u32[]{:S(2)}, u32[]{:S(2)}) collective-permute-start(f32[8,256]{1,0:T(8,128)S(1)} %get-tuple-element.18), channel_id=1, source_target_pairs={{0,1},{1,0},{2,3},{3,2},{4,5},{5,4},{6,7},{7,6},{8,9},{9,8},{10,11... | collective-permute-start | bytes 24584 | tf_op jit(solution)/shard_map/ppermute | solution.py:525
  10.0 3.1 %collective-permute-start.1 = (f32[8,256]{1,0:T(8,128)S(1)}, f32[8,256]{1,0:T(8,128)S(1)}, u32[]{:S(2)}, u32[]{:S(2)}) collective-permute-start(f32[8,256]{1,0:T(8,128)S(1)} %get-tuple-element.19), channel_id=1, source_target_pairs={{1,2},{2,1},{3,0},{0,3},{5,6},{6,5},{7,4},{4,7},{9,10},{10,9},{11,... | collective-permute-start | bytes 24584 | tf_op jit(solution)/shard_map/ppermute | solution.py:526
  13.5 5.6 %collective-permute-start.4 = (f32[64,128]{1,0:T(8,128)S(1)}, f32[64,128]{1,0:T(8,128)S(1)}, u32[]{:S(2)}, u32[]{:S(2)}) collective-permute-start(f32[64,128]{1,0:T(8,128)S(1)} %get-tuple-element.25), channel_id=1, source_target_pairs={{0,4},{4,0},{8,12},{12,8},{16,20},{20,16},{24,28},{28,24},{1,5},{5... | collective-permute-start | bytes 98312 | tf_op jit(solution)/shard_map/ppermute | solution.py:538
  13.6 6.9 %collective-permute-start.5 = (f32[64,128]{1,0:T(8,128)S(1)}, f32[64,128]{1,0:T(8,128)S(1)}, u32[]{:S(2)}, u32[]{:S(2)}) collective-permute-start(f32[64,128]{1,0:T(8,128)S(1)} %get-tuple-element.26), channel_id=1, source_target_pairs={{4,8},{8,4},{12,16},{16,12},{20,24},{24,20},{28,0},{0,28},{5,9},{9... | collective-permute-start | bytes 98312 | tf_op jit(solution)/shard_map/ppermute | solution.py:539

commit v3 on v2

--- a/solution.py
+++ b/solution.py
@@ -1,5 +1,3 @@
-import functools
-
 import jax
 import jax.numpy as jnp
 from jax import lax
@@ -7,10 +5,11 @@
 from jax.experimental.pallas import tpu as pltpu
 from jax.sharding import PartitionSpec as P
 
+
 TILE = 128
 time_step = 0.05
 STEP = 8
-BLOCK = (4, 4, 4)
+BLOCK = (4, 4, 8, 8)
 MERGE = 4
 CHUNK = 32
 VMEM_LIMIT = 8 << 20
@@ -52,7 +51,7 @@
     return (below[1] + above[1]) * scale, (below[2] + above[3]) * scale
 
 
-def cell_values(impedance, pressure, speed_x, speed_y, density, energy, lower, upper, from_right):
+def cell_update(impedance, pressure, speed_x, speed_y, density, energy, lower, upper, from_right):
     side_x = lower[0] + upper[0]
     side_y = lower[1] + upper[1]
     rise_y = upper[1] - lower[1]
@@ -65,42 +64,36 @@
     relaxation = (square + from_right(square)) - speed_x * sum_x - speed_y * sum_y
     left = (0.5 * time_step) * side_x
     right = (0.5 * time_step) * far_x
-    scale = 1.0 / (1.0 + (right - left))
     total = density * (energy + 0.5 * (speed_x * speed_x + speed_y * speed_y))
-    values = (
-        density * scale,
-        (density * speed_x + half_z * (sum_x - 4.0 * speed_x)) * scale,
-        (density * speed_y + half_z * (sum_y - 4.0 * speed_y)) * scale,
-        (total + (half_z * relaxation - (0.5 * time_step) * pressure * volume)) * scale,
+    conserved = (
+        density,
+        density * speed_x + half_z * (sum_x - 4.0 * speed_x),
+        density * speed_y + half_z * (sum_y - 4.0 * speed_y),
+        total + (half_z * relaxation - (0.5 * time_step) * pressure * volume),
     )
-    return values, left, right
-
-
-def remap_weights(shift, left, right):
+    return conserved, 0.5 / (1.0 + (right - left)), left, right
+
+
+def next_weights(shift, left, right):
     start = shift + left
-    stop = 1.0 + shift + right
-    centre = 0.5 * (start + stop)
-    low_own, high_own = jnp.maximum(start, 0.0), jnp.minimum(stop, 1.0)
-    span_own = jnp.maximum(high_own - low_own, 0.0)
-    low_next, high_next = jnp.maximum(start, 1.0), jnp.minimum(stop, 2.0)
-    span_next = jnp.maximum(high_next - low_next, 0.0)
-    return (
-        span_own,
-        span_own * (0.5 * (high_own + low_own) - centre),
-        span_next,
-        span_next * (0.5 * (high_next + low_next) - centre),
-    )
-
-
-def remapped_field(value, steepness, weights, from_left, from_right):
-    back = value - from_left(value)
-    fore = from_right(back)
-    mean = 0.5 * (back + fore)
-    rising = jnp.maximum(jnp.minimum(steepness * jnp.minimum(back, fore), mean), 0.0)
-    falling = jnp.minimum(jnp.maximum(steepness * jnp.maximum(back, fore), mean), 0.0)
-    slope = rising + falling
-    own = weights[0] * value + weights[1] * slope
-    return own + from_left(weights[2] * value + weights[3] * slope)
+    stop = (1.0 + shift) + right
+    low = jnp.maximum(start, 1.0)
+    span = jnp.maximum(stop - low, 0.0)
+    return 2.0 * span, (0.5 * span) * (low - start)
+
+
+def limited(back, fore, twice):
+    low = jnp.minimum(twice * jnp.maximum(back, fore), 0.0)
+    high = jnp.maximum(twice * jnp.minimum(back, fore), 0.0)
+    return jnp.minimum(jnp.maximum(back + fore, low), high)
+
+
+def remapped_field(conserved, scale, twice, weights, from_left, from_right):
+    half = conserved * scale
+    back = half - from_left(half)
+    slope = limited(back, from_right(back), twice)
+    onward = weights[0] * half + weights[1] * slope
+    return (conserved - onward) + from_left(onward)
 
 
 class Wide:
@@ -151,11 +144,42 @@
     return slice(h * TILE, (h + 1) * TILE)
 
 
+def wide_cells(z, p, sx, sy, rho, en, lower, upper, from_right):
+    parts = range(len(z.parts))
+    pieces = []
+    for h in parts:
+        lx, ly, ux, uy = (q.parts[h] for q in (*lower, *upper))
+        pieces.append((lx + ux, ly + uy, uy - ly, lx * lx + ux * ux + ly * ly + uy * uy))
+    far = [from_right(Wide(q)).parts for q in zip(*pieces)]
+    results = []
+    for h in parts:
+        order = iter([far[k][h] for k in range(4)])
+        results.append(
+            cell_update(
+                z.parts[h], p.parts[h], sx.parts[h], sy.parts[h], rho.parts[h], en.parts[h],
+                [q.parts[h] for q in lower], [q.parts[h] for q in upper], lambda _: next(order),
+            )
+        )
+    return results
+
+
+def wide_field(conserved, scale, twice, weights, left, right):
+    half = conserved * scale
+    back = half - left(half)
+    fore = right(back)
+    onward = []
+    for h in range(len(half.parts)):
+        slope = limited(back.parts[h], fore.parts[h], twice.parts[h])
+        onward.append(weights[0].parts[h] * half.parts[h] + weights[1].parts[h] * slope)
+    onward = Wide(onward)
+    return (conserved - onward) + left(onward)
+
+
 def block_kernel(
     rho_hbm, vel_hbm, en_hbm, mat_hbm, lim_hbm, shift_hbm, owner_hbm,
-    out_ref, first_ref, second_ref, edge_ref, rim_ref, near_ref, far_ref, row_ref,
+    first_ref, second_ref, edge_ref, rim_ref, near_ref, far_ref, row_ref,
     rho_ref, vel_ref, en_ref, mat_ref, lim_ref, shift_ref, owner_ref,
-    sums_ref, node_ref, press_ref, shifts_ref, edges_ref, sems, small_sems,
+    sums_ref, node_ref, press_ref, shifts_ref, edges_ref, kept_ref, sems, small_sems,
 ):
     rows, cols = rho_ref.shape
     halves = range(cols // TILE)
@@ -192,7 +216,7 @@
     def at_rows(i, offset=0):
         return pl.ds(pl.multiple_of(i * STEP, STEP) + offset, STEP)
 
-    def first_pass(i, _):
+    def first_pass(i):
         here = at_rows(i)
         rho = [rho_ref[here, lanes(h)] for h in halves]
         en = [en_ref[here, lanes(h)] for h in halves]
@@ -221,7 +245,7 @@
     def first_chunk(c, _):
         for copy in copies(c):
             copy.wait()
-        step = lambda j, _: first_pass(c * inner + j, 0)
+        step = lambda j, _: first_pass(c * inner + j)
         return lax.fori_loop(0, inner, step, 0, unroll=BLOCK[0])
 
     for s in range(4):
@@ -290,25 +314,31 @@
         p = Wide(press_ref[1, h, here, :] for h in halves)
         lower = [Wide(node_ref[d, h, here, :] for h in halves) for d in range(2)]
         upper = [Wide(node_ref[d, h, at_rows(i, 1), :] for h in halves) for d in range(2)]
-        steepness = Wide(lim_ref[here, lanes(h)].astype(jnp.float32) + 1.0 for h in halves)
         shift = shifts_ref[here, :]
-        values, dl, dr = wide_cells(z, p, sx, sy, rho, en, lower, upper, right)
-        weights = [remap_weights(shift, dl.parts[h], dr.parts[h]) for h in halves]
-        weights = [Wide(w) for w in zip(*weights)]
-        for f, value in enumerate(values):
-            done = wide_field(value, steepness, weights, left, right)
-            for h in halves:
-                out_ref[f, here, lanes(h)] = done.parts[h]
+        cells = wide_cells(z, p, sx, sy, rho, en, lower, upper, right)
+        for h, (conserved, scale, ends_left, ends_right) in enumerate(cells):
+            for k, value in enumerate((*conserved[1:], scale, *next_weights(shift, ends_left, ends_right))):
+                kept_ref[k, h, here, :] = value
+        return 0
+
+    def fourth_pass(i, _):
+        here = at_rows(i)
+        twice = Wide(2.0 * lim_ref[here, lanes(h)].astype(jnp.float32) + 2.0 for h in halves)
+        kept = [Wide(kept_ref[k, h, here, :] for h in halves) for k in range(6)]
+        rho = Wide(rho_ref[here, lanes(h)] for h in halves)
+        for f, conserved in enumerate((rho, *kept[:3])):
+            done = wide_field(conserved, kept[3], twice, kept[4:], left, right)
+            spot = pl.ds(pl.multiple_of(f * rows + i * STEP, STEP), STEP)
             ends = done.parts[0], done.parts[-1]
-            spot = pl.ds(pl.multiple_of(f * rows + i * STEP, STEP), STEP)
             first_ref[spot, :] = jnp.where(even_x, ends[1], ends[0])
             second_ref[spot, :] = jnp.where(even_x, ends[0], ends[1])
         return 0
 
     lax.fori_loop(0, rows // STEP, third_pass, 0, unroll=BLOCK[2])
-
-
-def rim_kernel(near_ref, far_ref, kept_ref, edge_ref, rows_ref, first_ref, second_ref, corner_ref):
+    lax.fori_loop(0, rows // STEP, fourth_pass, 0, unroll=BLOCK[3])
+
+
+def rim_kernel(near_ref, far_ref, kept_ref, edge_ref, first_ref, second_ref, corner_ref):
     cols = near_ref.shape[-1]
     halves = range(cols // TILE)
     even_x = lax.axis_index("gx") % 2 == 0
@@ -339,14 +369,14 @@
     fresh = [Wide(q) for q in zip(*fresh)]
     lower = [Wide(jnp.where(bottom, x, y) for x, y in zip(a.parts, b.parts)) for a, b in zip(fresh, joint)]
     upper = [Wide(jnp.where(bottom, y, x) for x, y in zip(a.parts, b.parts)) for a, b in zip(fresh, joint)]
-    values, dl, dr = wide_cells(z, p, sx, sy, rho, en, lower, upper, right)
-    weights = [remap_weights(shift.parts[h], dl.parts[h], dr.parts[h]) for h in halves]
+    cells = wide_cells(z, p, sx, sy, rho, en, lower, upper, right)
+    weights = [next_weights(shift.parts[h], *cells[h][2:]) for h in halves]
     weights = [Wide(w) for w in zip(*weights)]
-    steepness = Wide(q + 1.0 for q in lim.parts)
-    for f, value in enumerate(values):
-        done = wide_field(value, steepness, weights, left, right)
-        for h in halves:
-            rows_ref[2 * f : 2 * f + 2, lanes(h)] = done.parts[h][0:2, :]
+    twice = Wide(2.0 * q + 2.0 for q in lim.parts)
+    scale = Wide(c[1] for c in cells)
+    for f in range(4):
+        conserved = Wide(c[0][f] for c in cells)
+        done = wide_field(conserved, scale, twice, weights, left, right)
         ends = done.parts[0][0:2, :], done.parts[-1][0:2, :]
         first_ref[2 * f : 2 * f + 2, :] = jnp.where(even_x, ends[1], ends[0])
         second_ref[2 * f : 2 * f + 2, :] = jnp.where(even_x, ends[0], ends[1])
@@ -367,21 +397,20 @@
         second_ref[spot, :] = jnp.where(even_x, left_edge, right_edge)
 
 
-def edge_kernel(edge_ref, corner_ref, first_ref, second_ref, row_ref, patch_ref):
+def edge_kernel(edge_ref, corner_ref, from_near_ref, from_far_ref, row_ref, patch_ref):
     rows = patch_ref.shape[0]
     even_x = lax.axis_index("gx") % 2 == 0
     span = 4 * EDGE
 
     def window(k):
         spot = slice(8 + k * EDGE, 8 + (k + 1) * EDGE)
-        from_near, from_far = first_ref[spot, :], second_ref[spot, :]
         own, at = (edge_ref, 2 * k * EDGE) if k < RAW else (corner_ref, 0)
         return jnp.concatenate(
             [
-                jnp.where(even_x, from_far, from_near),
+                jnp.where(even_x, from_far_ref[spot, :], from_near_ref[spot, :]),
                 own[at + EDGE : at + 2 * EDGE, :],
                 own[at : at + EDGE, :],
-                jnp.where(even_x, from_near, from_far),
+                jnp.where(even_x, from_near_ref[spot, :], from_far_ref[spot, :]),
             ],
             axis=0,
         )
@@ -398,74 +427,71 @@
     lane = lax.broadcasted_iota(jnp.int32, (span, rows), 1)
     under = [jnp.where(lane == 0, b, pltpu.roll(a, 1, 1)) for a, b in zip(own, below)]
     over = [jnp.where(lane == rows - 1, b, pltpu.roll(a, rows - 1, 1)) for a, b in zip(own, above)]
-    values, dl, dr = cell_values(
+    conserved, scale, ends_left, ends_right = cell_update(
         z, p, sx, sy, rho, en, nodes(under, own), nodes(own, over), right
     )
-    weights = remap_weights(row_ref[0:1, :], dl, dr)
-    fields = [remapped_field(v, lim + 1.0, weights, left, right) for v in values]
+    weights = next_weights(row_ref[0:1, :], ends_left, ends_right)
+    fields = [remapped_field(q, scale, 2.0 * lim + 2.0, weights, left, right) for q in conserved]
     patch_ref[...] = jnp.concatenate(fields, axis=0).T
 
 
 def merge_kernel(
-    field_ref, rows_ref, first_ref, second_ref, small_first_ref, small_second_ref, patch_ref,
+    first_ref, second_ref, from_near_ref, from_far_ref,
+    rim_first_ref, rim_second_ref, rim_near_ref, rim_far_ref, patch_ref,
     row_ref, out_hbm, out_ref, sems,
 ):
-    rows = field_ref.shape[1]
-    even_x = lax.axis_index("gx") % 2 == 0
+    rows = out_ref.shape[1]
     span = 4 * EDGE
     chunks, inner = rows // CHUNK, CHUNK // STEP
-
+    even_x = lax.axis_index("gx") % 2 == 0
     to_left, to_right = row_ref[1:2, :], row_ref[2:3, :]
 
-    def put(here, row, patch, pick_own, pick_sent):
+    def put(here, row, patch, pick):
         goes_left, goes_right = row < to_left, row >= rows - to_right
         lane = lax.broadcasted_iota(jnp.int32, patch.shape, 1)
         head, tail = lane < 3, lane >= TILE - 2
         for f in range(4):
             at_left = pltpu.roll(patch, (-(span * f + EDGE)) % TILE, 1)
             at_right = pltpu.roll(patch, (-(span * f + 3 * EDGE)) % TILE, 1)
-            from_near, from_far = pick_sent(f)
-            own_0 = jnp.where(head, at_left, pick_own(f, 0))
-            own_1 = jnp.where(tail, at_right, pick_own(f, 1))
-            left_tile = jnp.where(tail, at_left, jnp.where(even_x, from_far, from_near))
-            right_tile = jnp.where(head, at_right, jnp.where(even_x, from_near, from_far))
+            first, second, near, far = pick(f)
+            own_0 = jnp.where(head, at_left, jnp.where(even_x, second, first))
+            own_1 = jnp.where(tail, at_right, jnp.where(even_x, first, second))
+            before = jnp.where(tail, at_left, jnp.where(even_x, far, near))
+            after = jnp.where(head, at_right, jnp.where(even_x, near, far))
             out_ref[f, here, lanes(0)] = jnp.where(
-                goes_right, left_tile, jnp.where(goes_left, own_1, own_0)
+                goes_right, before, jnp.where(goes_left, own_1, own_0)
             )
             out_ref[f, here, lanes(1)] = jnp.where(
-                goes_right, own_0, jnp.where(goes_left, right_tile, own_1)
+                goes_right, own_0, jnp.where(goes_left, after, own_1)
             )
 
     row_in = lax.broadcasted_iota(jnp.int32, (STEP, TILE), 0)
 
-    def one(i, _):
+    whole = (first_ref, second_ref, from_near_ref, from_far_ref)
+    rims = (rim_first_ref, rim_second_ref, rim_near_ref, rim_far_ref)
+
+    def one(i):
         here = pl.ds(pl.multiple_of(i * STEP, STEP), STEP)
 
-        def sent(f):
+        def pick(f):
             spot = pl.ds(pl.multiple_of(f * rows + i * STEP, STEP), STEP)
-            return first_ref[spot, :], second_ref[spot, :]
-
-        row = (row_in + i * STEP).astype(jnp.float32)
-        put(here, row, patch_ref[here, :], lambda f, h: field_ref[f, here, lanes(h)], sent)
+            return [ref[spot, :] for ref in whole]
+
+        put(here, (row_in + i * STEP).astype(jnp.float32), patch_ref[here, :], pick)
         return 0
 
     def rim(r):
         row = r * (rows - 1)
         here = slice(row, row + 1)
-
-        def sent(f):
-            spot = slice(2 * f + r, 2 * f + r + 1)
-            return small_first_ref[spot, :], small_second_ref[spot, :]
-
-        own = lambda f, h: rows_ref[2 * f + r : 2 * f + r + 1, lanes(h)]
-        put(here, jnp.full((1, TILE), float(row)), patch_ref[here, :], own, sent)
+        pick = lambda f: [ref[2 * f + r : 2 * f + r + 1, :] for ref in rims]
+        put(here, jnp.full((1, TILE), float(row)), patch_ref[here, :], pick)
 
     def copy(c):
         part = pl.ds(pl.multiple_of(c * CHUNK, CHUNK), CHUNK)
         return pltpu.make_async_copy(out_ref.at[:, part, :], out_hbm.at[:, 0, part, :], sems.at[c])
 
     def chunk(c, _):
-        lax.fori_loop(0, inner, lambda j, _: one(c * inner + j, 0), 0, unroll=MERGE)
+        lax.fori_loop(0, inner, lambda j, _: one(c * inner + j), 0, unroll=MERGE)
         pl.when(c == 0)(lambda: rim(0))
         pl.when(c == chunks - 1)(lambda: rim(1))
         copy(c).start()
@@ -488,14 +514,14 @@
     chunks = rows // CHUNK
     stay = lambda array: pltpu.with_memory_space_constraint(array, pltpu.HBM)
 
-    field, first, second, edge, kept, near, far, per_row = pl.pallas_call(
+    tile = shape(4 * rows, TILE)
+    first, second, edge, kept, near, far, per_row = pl.pallas_call(
         block_kernel,
         in_specs=[hbm] * 7,
-        out_specs=[vmem] * 8,
+        out_specs=[vmem] * 7,
         out_shape=[
-            shape(4, rows, cols),
-            shape(4 * rows, TILE),
-            shape(4 * rows, TILE),
+            tile,
+            tile,
             shape(2 * RAW * EDGE, TILE),
             shape(14, 8, cols),
             shape(8, cols),
@@ -515,28 +541,29 @@
             pltpu.VMEM((2, 2, rows, TILE), f32),
             pltpu.VMEM((TILE, TILE), f32),
             pltpu.VMEM((rows, TILE), f32),
+            pltpu.VMEM((6, 2, rows, TILE), f32),
             pltpu.SemaphoreType.DMA((5, chunks)),
             pltpu.SemaphoreType.DMA((2,)),
         ],
         compiler_params=params,
         name="block",
     )(*map(stay, (density, velocity, energy, material, limiter, tile_shift, owners.reshape(-1, TILE))))
-    first = lax.ppermute(first, "gx", near_pairs(gx))
+    from_near = lax.ppermute(first, "gx", near_pairs(gx))
+    from_far = lax.ppermute(second, "gx", far_pairs(gx))
     near = lax.ppermute(near, "gy", near_pairs(gy))
     far = lax.ppermute(far, "gy", far_pairs(gy))
-    second = lax.ppermute(second, "gx", far_pairs(gx))
 
     small = shape(8 + (RAW + 1) * EDGE, TILE)
-    outer_rows, small_first, small_second, corner = pl.pallas_call(
+    small_first, small_second, corner = pl.pallas_call(
         rim_kernel,
         in_specs=[vmem] * 4,
-        out_specs=[vmem] * 4,
-        out_shape=[shape(8, cols), small, small, shape(2 * EDGE, TILE)],
+        out_specs=[vmem] * 3,
+        out_shape=[small, small, shape(2 * EDGE, TILE)],
         compiler_params=params,
         name="rim",
     )(near, far, kept, edge)
-    small_first = lax.ppermute(small_first, "gx", near_pairs(gx))
-    small_second = lax.ppermute(small_second, "gx", far_pairs(gx))
+    small_near = lax.ppermute(small_first, "gx", near_pairs(gx))
+    small_far = lax.ppermute(small_second, "gx", far_pairs(gx))
 
     patch = pl.pallas_call(
         edge_kernel,
@@ -545,56 +572,20 @@
         out_shape=shape(rows, TILE),
         compiler_params=params,
         name="edge",
-    )(edge, corner, small_first, small_second, per_row)
+    )(edge, corner, small_near, small_far, per_row)
 
     return pl.pallas_call(
         merge_kernel,
-        in_specs=[vmem] * 8,
+        in_specs=[vmem] * 10,
         out_specs=hbm,
         out_shape=shape(4, planes, rows, cols),
         scratch_shapes=[pltpu.VMEM((4, rows, cols), f32), pltpu.SemaphoreType.DMA((chunks,))],
         compiler_params=params,
         name="merge",
     )(
-        field, outer_rows, first, second, small_first, small_second, patch, per_row,
+        first, second, from_near, from_far,
+        small_first, small_second, small_near, small_far, patch, per_row,
     )
-
-
-def wide_cells(z, p, sx, sy, rho, en, lower, upper, from_right):
-    halves = range(len(z.parts))
-    pieces = []
-    for h in halves:
-        lx, ly, ux, uy = (q.parts[h] for q in (*lower, *upper))
-        pieces.append((lx + ux, ly + uy, uy - ly, lx * lx + ux * ux + ly * ly + uy * uy))
-    far = [from_right(Wide(q)).parts for q in zip(*pieces)]
-    results = []
-    for h in halves:
-        queue = [far[k][h] for k in (0, 1, 2, 3)]
-        order = iter(queue)
-        results.append(
-            cell_values(
-                z.parts[h], p.parts[h], sx.parts[h], sy.parts[h], rho.parts[h], en.parts[h],
-                [q.parts[h] for q in lower], [q.parts[h] for q in upper], lambda _: next(order),
-            )
-        )
-    values = [Wide(results[h][0][f] for h in halves) for f in range(4)]
-    return values, Wide(r[1] for r in results), Wide(r[2] for r in results)
-
-
-def wide_field(value, steepness, weights, left, right):
-    back = value - left(value)
-    fore = right(back)
-    owns, nexts = [], []
-    for h in range(len(value.parts)):
-        b, f, k = back.parts[h], fore.parts[h], steepness.parts[h]
-        mean = 0.5 * (b + f)
-        rising = jnp.maximum(jnp.minimum(k * jnp.minimum(b, f), mean), 0.0)
-        falling = jnp.minimum(jnp.maximum(k * jnp.maximum(b, f), mean), 0.0)
-        slope = rising + falling
-        w = [q.parts[h] for q in weights]
-        owns.append(w[0] * value.parts[h] + w[1] * slope)
-        nexts.append(w[2] * value.parts[h] + w[3] * slope)
-    return Wide(owns) + left(Wide(nexts))
 
 
 def solution(mesh):

time: 22.2 us -> 21.9 us (0.986)
  Pallas kernels: 5.41 us -> 5.03 us
    pallas_call x3, Pallas kernels: 5.1 us -> 4.74 us  [the longest x1 3.07 us: on_device(): pl.pallas_call(block_kernel, in_specs=[hbm] * 7, out_specs=[vmem] * 7, ou...]
where the time goes in v3:
time: 21.9 us; the launch traced here: 21.7 us
  starting transfers between devices  10.2 us (47%)
  waiting for transfers between devices  6.44 us (29%)
  Pallas kernels  5.03 us (23%)
    ppermute x1, waiting for transfers between devices, on_device(): small_near = lax.ppermute(small_first, 'gx', near_pairs(gx))  3.63 us
    ppermute x1, starting transfers between devices, on_device(): from_far = lax.ppermute(second, 'gx', far_pairs(gx))  3.54 us
    pallas_call x1, Pallas kernels, on_device(): pl.pallas_call(block_kernel, in_specs=[hbm] * 7, out_specs=[vmem] * 7, ou...  3.07 us
    ppermute x1, starting transfers between devices, on_device(): from_near = lax.ppermute(first, 'gx', near_pairs(gx))  3.06 us
    ppermute x1, starting transfers between devices, on_device(): small_far = lax.ppermute(small_second, 'gx', far_pairs(gx))  1.9 us
    ppermute x1, starting transfers between devices, on_device(): far = lax.ppermute(far, 'gy', far_pairs(gy))  1.6 us
    ppermute x1, waiting for transfers between devices, on_device(): far = lax.ppermute(far, 'gy', far_pairs(gy))  1.47 us
    ppermute x1, waiting for transfers between devices, on_device(): small_far = lax.ppermute(small_second, 'gx', far_pairs(gx))  1.33 us
  transfers between devices with their start and end apart: 6, of which 3 were waited for; matrix products, arithmetic and copies ran while one was open for 0% of the time, Pallas kernels for 3%

profile of v3, /device:TPU:0, one launch (start us, length us, event | category | flops | bytes accessed | tf_op | source)
XLA Modules:
  0.0 21.7 jit_solution(3744357886803900691)
XLA Ops:
  0.0 3.1 %block.1 = (f32[512,128]{1,0:T(8,128)S(1)}, f32[512,128]{1,0:T(8,128)S(1)}, f32[96,128]{1,0:T(8,128)S(1)}, f32[14,8,256]{2,1,0:T(8,128)S(1)}, f32[8,256]{1,0:T(8...) custom-call(f32[1,128,256]{2,1,0:T(8,128)} %rho_hbm.1, f32[2,1,128,256]{3,2,1,0:T(8,128)} %vel_hbm.1, ...), custom_call_target="tpu_custom_call" | custom-call | tf_op jit(solution)/shard_map/block/pallas_call | solution.py:518
  3.1 3.1 %collective-permute-start = (f32[512,128]{1,0:T(8,128)S(1)}, f32[512,128]{1,0:T(8,128)S(1)}, u32[]{:S(2)}, u32[]{:S(2)}) collective-permute-start(f32[512,128]{1,0:T(8,128)S(1)} %get-tuple-element.15.first_ref), channel_id=1, source_target_pairs={{0,4},{4,0},{8,12},{12,8},{16,20},{20,16},{24,28},{28,24},{1,5},{5... | collective-permute-start | bytes 786440 | tf_op jit(solution)/shard_map/ppermute | solution.py:551
  6.1 3.5 %collective-permute-start.1 = (f32[512,128]{1,0:T(8,128)S(1)}, f32[512,128]{1,0:T(8,128)S(1)}, u32[]{:S(2)}, u32[]{:S(2)}) collective-permute-start(f32[512,128]{1,0:T(8,128)S(1)} %get-tuple-element.16.second_ref), channel_id=1, source_target_pairs={{4,8},{8,4},{12,16},{16,12},{20,24},{24,20},{28,0},{0,28},{5,9},{9... | collective-permute-start | bytes 786440 | tf_op jit(solution)/shard_map/ppermute | solution.py:552
  9.7 0.0 collective-permute-start.2
  9.7 1.6 %collective-permute-start.3 = (f32[8,256]{1,0:T(8,128)S(1)}, f32[8,256]{1,0:T(8,128)S(1)}, u32[]{:S(2)}, u32[]{:S(2)}) collective-permute-start(f32[8,256]{1,0:T(8,128)S(1)} %get-tuple-element.18), channel_id=1, source_target_pairs={{1,2},{2,1},{3,0},{0,3},{5,6},{6,5},{7,4},{4,7},{9,10},{10,9},{11,... | collective-permute-start | bytes 24584 | tf_op jit(solution)/shard_map/ppermute | solution.py:554
  11.3 0.0 collective-permute-done.2.near_ref
  11.3 1.5 %collective-permute-done.3.far_ref = f32[8,256]{1,0:T(8,128)S(1)} collective-permute-done((f32[8,256]{1,0:T(8,128)S(1)}, f32[8,256]{1,0:T(8,128)S(1)}, u32[]{:S(2)}, u32[]{:S(2)}) %collective-permute-start.3) | collective-permute-done | bytes 8224 | tf_op jit(solution)/shard_map/ppermute | solution.py:554
  12.8 0.4 %rim.1 = (f32[64,128]{1,0:T(8,128)S(1)}, f32[64,128]{1,0:T(8,128)S(1)}, f32[16,128]{1,0:T(8,128)S(1)}) custom-call(f32[8,256]{1,0:T(8,128)S(1)} %collective-permute-done.2.near_ref, f32[8,256]{1,0:T(8,128)S(1)} %collective-permute-done.3.far_ref, f32[14,8,256]{2,1,0:T(8,128)S(1)} %get-tuple-element.19.kept_ref, f32[96,128]{1,0:T(8,128)S(1)} %get-tuple-element.20.edge_ref), custom_call_target="tpu_custom_call" | custom-call | tf_op jit(solution)/shard_map/rim/pallas_call | solution.py:557
  13.2 0.1 collective-permute-start.4
  13.2 1.9 %collective-permute-start.5 = (f32[64,128]{1,0:T(8,128)S(1)}, f32[64,128]{1,0:T(8,128)S(1)}, u32[]{:S(2)}, u32[]{:S(2)}) collective-permute-start(f32[64,128]{1,0:T(8,128)S(1)} %get-tuple-element.22.rim_second_ref), channel_id=1, source_target_pairs={{4,8},{8,4},{12,16},{16,12},{20,24},{24,20},{28,0},{0,28},{5,9},{9... | collective-permute-start | bytes 98312 | tf_op jit(solution)/shard_map/ppermute | solution.py:566
  15.1 3.6 %collective-permute-done.4.from_near_ref.rim_near_ref = f32[64,128]{1,0:T(8,128)S(1)} collective-permute-done((f32[64,128]{1,0:T(8,128)S(1)}, f32[64,128]{1,0:T(8,128)S(1)}, u32[]{:S(2)}, u32[]{:S(2)}) %collective-permute-start.4) | collective-permute-done | bytes 32800 | tf_op jit(solution)/shard_map/ppermute | solution.py:565
  18.8 1.3 %collective-permute-done.5.from_far_ref.rim_far_ref = f32[64,128]{1,0:T(8,128)S(1)} collective-permute-done((f32[64,128]{1,0:T(8,128)S(1)}, f32[64,128]{1,0:T(8,128)S(1)}, u32[]{:S(2)}, u32[]{:S(2)}) %collective-permute-start.5) | collective-permute-done | bytes 32800 | tf_op jit(solution)/shard_map/ppermute | solution.py:566
  20.1 0.3 %edge.1.patch_ref = f32[128,128]{1,0:T(8,128)S(1)} custom-call(f32[96,128]{1,0:T(8,128)S(1)} %get-tuple-element.20.edge_ref, f32[16,128]{1,0:T(8,128)S(1)} %get-tuple-element.23.corner_ref, f32[64,128]{1,0:T(8,128)S(1)} %collective-permute-done.4.from_near_ref.rim_near_ref, f32[64,128]{1,0:T(8,128)S(1)} %collective-permute-done.5.from_far_ref.rim_far_ref, ...), custom_call_target="tpu_custom_call" | custom-call | tf_op jit(solution)/shard_map/edge/pallas_call | solution.py:568
  20.4 0.0 collective-permute-done.from_near_ref
  20.4 0.0 collective-permute-done.1.from_far_ref
  20.4 1.3 %merge.1 = f32[4,1,128,256]{3,2,1,0:T(8,128)} custom-call(f32[512,128]{1,0:T(8,128)S(1)} %get-tuple-element.15.first_ref, f32[512,128]{1,0:T(8,128)S(1)} %get-tuple-element.16.second_ref, f32[512,128]{1,0:T(8,128)S(1)} %collective-permute-done.from_near_ref, f32[512,128]{1,0:T(8,128)S(1)} %collective-permute-done.1.from_far_ref, ...), custom_call_target="tpu_custom_call" | custom-call | tf_op jit(solution)/shard_map/merge/pallas_call | solution.py:577
Async XLA Ops:
  3.1 17.3 %collective-permute-start = (f32[512,128]{1,0:T(8,128)S(1)}, f32[512,128]{1,0:T(8,128)S(1)}, u32[]{:S(2)}, u32[]{:S(2)}) collective-permute-start(f32[512,128]{1,0:T(8,128)S(1)} %get-tuple-element.15.first_ref), channel_id=1, source_target_pairs={{0,4},{4,0},{8,12},{12,8},{16,20},{20,16},{24,28},{28,24},{1,5},{5... | collective-permute-start | bytes 786440 | tf_op jit(solution)/shard_map/ppermute | solution.py:551
  6.1 14.3 %collective-permute-start.1 = (f32[512,128]{1,0:T(8,128)S(1)}, f32[512,128]{1,0:T(8,128)S(1)}, u32[]{:S(2)}, u32[]{:S(2)}) collective-permute-start(f32[512,128]{1,0:T(8,128)S(1)} %get-tuple-element.16.second_ref), channel_id=1, source_target_pairs={{4,8},{8,4},{12,16},{16,12},{20,24},{24,20},{28,0},{0,28},{5,9},{9... | collective-permute-start | bytes 786440 | tf_op jit(solution)/shard_map/ppermute | solution.py:552
  9.7 1.6 %collective-permute-start.2 = (f32[8,256]{1,0:T(8,128)S(1)}, f32[8,256]{1,0:T(8,128)S(1)}, u32[]{:S(2)}, u32[]{:S(2)}) collective-permute-start(f32[8,256]{1,0:T(8,128)S(1)} %get-tuple-element.17), channel_id=1, source_target_pairs={{0,1},{1,0},{2,3},{3,2},{4,5},{5,4},{6,7},{7,6},{8,9},{9,8},{10,11... | collective-permute-start | bytes 24584 | tf_op jit(solution)/shard_map/ppermute | solution.py:553
  9.7 3.1 %collective-permute-start.3 = (f32[8,256]{1,0:T(8,128)S(1)}, f32[8,256]{1,0:T(8,128)S(1)}, u32[]{:S(2)}, u32[]{:S(2)}) collective-permute-start(f32[8,256]{1,0:T(8,128)S(1)} %get-tuple-element.18), channel_id=1, source_target_pairs={{1,2},{2,1},{3,0},{0,3},{5,6},{6,5},{7,4},{4,7},{9,10},{10,9},{11,... | collective-permute-start | bytes 24584 | tf_op jit(solution)/shard_map/ppermute | solution.py:554
  13.2 5.6 %collective-permute-start.4 = (f32[64,128]{1,0:T(8,128)S(1)}, f32[64,128]{1,0:T(8,128)S(1)}, u32[]{:S(2)}, u32[]{:S(2)}) collective-permute-start(f32[64,128]{1,0:T(8,128)S(1)} %get-tuple-element.21.rim_first_ref), channel_id=1, source_target_pairs={{0,4},{4,0},{8,12},{12,8},{16,20},{20,16},{24,28},{28,24},{1,5},{5... | collective-permute-start | bytes 98312 | tf_op jit(solution)/shard_map/ppermute | solution.py:565
  13.2 6.9 %collective-permute-start.5 = (f32[64,128]{1,0:T(8,128)S(1)}, f32[64,128]{1,0:T(8,128)S(1)}, u32[]{:S(2)}, u32[]{:S(2)}) collective-permute-start(f32[64,128]{1,0:T(8,128)S(1)} %get-tuple-element.22.rim_second_ref), channel_id=1, source_target_pairs={{4,8},{8,4},{12,16},{16,12},{20,24},{24,20},{28,0},{0,28},{5,9},{9... | collective-permute-start | bytes 98312 | tf_op jit(solution)/shard_map/ppermute | solution.py:566

commit v4 on v3

--- a/solution.py
+++ b/solution.py
@@ -9,9 +9,11 @@
 TILE = 128
 time_step = 0.05
 STEP = 8
-BLOCK = (4, 4, 8, 8)
-MERGE = 4
-CHUNK = 32
+BLOCK = (8, 8, 16, 8)
+MERGE = 8
+EDGES = 4
+LOAD = 64
+CHUNK = 64
 VMEM_LIMIT = 8 << 20
 EDGE = 8
 RAW = 6
@@ -177,20 +179,18 @@
 
 def block_kernel(
     rho_hbm, vel_hbm, en_hbm, mat_hbm, lim_hbm, shift_hbm, owner_hbm,
-    first_ref, second_ref, edge_ref, rim_ref, near_ref, far_ref, row_ref,
-    rho_ref, vel_ref, en_ref, mat_ref, lim_ref, shift_ref, owner_ref,
-    sums_ref, node_ref, press_ref, shifts_ref, edges_ref, kept_ref, sems, small_sems,
+    first_ref, second_ref, near_ref, far_ref, rho_ref, vel_ref, en_ref, mat_ref, lim_ref, owner_ref,
+    sums_ref, node_ref, press_ref, shifts_ref, shift_ref, kept_ref, sems, small_sems,
 ):
     rows, cols = rho_ref.shape
     halves = range(cols // TILE)
-    last = len(halves) - 1
     even_x = lax.axis_index("gx") % 2 == 0
     even_y = lax.axis_index("gy") % 2 == 0
     pad = 8
-    chunks, inner = rows // CHUNK, CHUNK // STEP
+    chunks, inner = rows // LOAD, LOAD // STEP
 
     def copies(c):
-        part = pl.ds(pl.multiple_of(c * CHUNK, CHUNK), CHUNK)
+        part = pl.ds(pl.multiple_of(c * LOAD, LOAD), LOAD)
         return [
             pltpu.make_async_copy(rho_hbm.at[0, part, :], rho_ref.at[part, :], sems.at[0, c]),
             pltpu.make_async_copy(en_hbm.at[0, part, :], en_ref.at[part, :], sems.at[1, c]),
@@ -232,14 +232,6 @@
         for s, total in enumerate(totals):
             for h in halves:
                 sums_ref[s, h, at_rows(i, pad), :] = total.parts[h]
-        lim = [lim_ref[here, lanes(h)].astype(jnp.float32) for h in (0, last)]
-        mats = [mat[0].astype(jnp.float32), mat[-1].astype(jnp.float32)]
-        edge = jnp.zeros((STEP, TILE), jnp.float32)
-        ends = ((rho[0], rho[-1]), (sx[0], sx[-1]), (sy[0], sy[-1]), (en[0], en[-1]), mats, lim)
-        for k, (start, stop) in enumerate(ends):
-            turned = pltpu.roll(jnp.where(lane < TILE // 2, start, stop), (2 * k + 1) * EDGE, 1)
-            edge = jnp.where(lane >= 2 * k * EDGE, turned, edge)
-        edges_ref[here, :] = edge
         return 0
 
     def first_chunk(c, _):
@@ -266,13 +258,6 @@
     for copy in small:
         copy.wait()
     shifts_ref[...] = jnp.broadcast_to(shift_ref[...], (TILE, TILE)).T
-    column, count = lax.axis_index("gx"), lax.axis_size("gx")
-    owner = owner_ref[...]
-    row_ref[0:1, :] = shift_ref[...]
-    for k, which in enumerate(((column + count - 1) % count, (column + 1) % count)):
-        hits = jnp.where(owner == which, 1.0, 0.0)
-        total = jnp.sum(jnp.sum(hits, axis=1, keepdims=True), axis=0, keepdims=True)
-        row_ref[k + 1 : k + 2, :] = jnp.broadcast_to(total, (1, TILE))
     lax.fori_loop(0, rows // STEP, second_pass, 0, unroll=BLOCK[1])
     for h in halves:
         for d in range(2):
@@ -288,22 +273,6 @@
             top, bottom = pick(rows - 1), pick(0)
             near_ref[k : k + 1, lanes(h)] = jnp.where(even_y, top, bottom)
             far_ref[k : k + 1, lanes(h)] = jnp.where(even_y, bottom, top)
-    for r, row in enumerate((0, rows - 1)):
-        at, to = slice(row, row + 1), slice(r, r + 1)
-        joint = slice(1, 2) if r == 0 else slice(rows - 1, rows)
-        for h in halves:
-            kept = [
-                press_ref[0, h, at, :], press_ref[1, h, at, :],
-                vel_ref[0, at, lanes(h)], vel_ref[1, at, lanes(h)],
-                rho_ref[at, lanes(h)], en_ref[at, lanes(h)],
-                lim_ref[at, lanes(h)].astype(jnp.float32), shifts_ref[at, :],
-                *(sums_ref[s, h, pad + row : pad + row + 1, :] for s in range(4)),
-                *(node_ref[d, h, joint, :] for d in range(2)),
-            ]
-            for k, value in enumerate(kept):
-                rim_ref[k, to, lanes(h)] = value
-
-    edge_ref[...] = edges_ref[...].T[0 : 2 * RAW * EDGE, :]
 
     def third_pass(i, _):
         here = at_rows(i)
@@ -336,6 +305,54 @@
 
     lax.fori_loop(0, rows // STEP, third_pass, 0, unroll=BLOCK[2])
     lax.fori_loop(0, rows // STEP, fourth_pass, 0, unroll=BLOCK[3])
+
+
+def rows_kernel(
+    rho_ref, vel_ref, en_ref, mat_ref, lim_ref, owner_ref, sums_ref, node_ref, press_ref, shifts_ref,
+    edge_ref, rim_ref, row_ref, edges_ref,
+):
+    rows, cols = rho_ref.shape
+    halves = range(cols // TILE)
+    pad = 8
+    lane = lax.broadcasted_iota(jnp.int32, (STEP, TILE), 1)
+
+    def edges(i, _):
+        here = pl.ds(pl.multiple_of(i * STEP, STEP), STEP)
+        edge = jnp.zeros((STEP, TILE), jnp.float32)
+        ends = [
+            [ref[(*at, here, lanes(h))].astype(jnp.float32) for h in (0, len(halves) - 1)]
+            for ref, *at in ((rho_ref,), (vel_ref, 0), (vel_ref, 1), (en_ref,), (mat_ref,), (lim_ref,))
+        ]
+        for k, (start, stop) in enumerate(ends):
+            turned = pltpu.roll(jnp.where(lane < TILE // 2, start, stop), (2 * k + 1) * EDGE, 1)
+            edge = jnp.where(lane >= 2 * k * EDGE, turned, edge)
+        edges_ref[here, :] = edge
+        return 0
+
+    lax.fori_loop(0, rows // STEP, edges, 0, unroll=EDGES)
+    row_ref[0:1, :] = shifts_ref[...].T[0:1, :]
+    column, count = lax.axis_index("gx"), lax.axis_size("gx")
+    owner = owner_ref[...]
+    for k, which in enumerate(((column + count - 1) % count, (column + 1) % count)):
+        hits = jnp.where(owner == which, 1.0, 0.0)
+        total = jnp.sum(jnp.sum(hits, axis=1, keepdims=True), axis=0, keepdims=True)
+        row_ref[k + 1 : k + 2, :] = jnp.broadcast_to(total, (1, TILE))
+    for r, row in enumerate((0, rows - 1)):
+        at, to = slice(row, row + 1), slice(r, r + 1)
+        joint = slice(1, 2) if r == 0 else slice(rows - 1, rows)
+        for h in halves:
+            kept = [
+                press_ref[0, h, at, :], press_ref[1, h, at, :],
+                vel_ref[0, at, lanes(h)], vel_ref[1, at, lanes(h)],
+                rho_ref[at, lanes(h)], en_ref[at, lanes(h)],
+                lim_ref[at, lanes(h)].astype(jnp.float32), shifts_ref[at, :],
+                *(sums_ref[s, h, pad + row : pad + row + 1, :] for s in range(4)),
+                *(node_ref[d, h, joint, :] for d in range(2)),
+            ]
+            for k, value in enumerate(kept):
+                rim_ref[k, to, lanes(h)] = value
+
+    edge_ref[...] = edges_ref[...].T[0 : 2 * RAW * EDGE, :]
 
 
 def rim_kernel(near_ref, far_ref, kept_ref, edge_ref, first_ref, second_ref, corner_ref):
@@ -511,36 +528,34 @@
     hbm = pl.BlockSpec(memory_space=pltpu.HBM)
     shape = lambda *dims: jax.ShapeDtypeStruct(dims, f32)
     params = pltpu.CompilerParams(vmem_limit_bytes=VMEM_LIMIT)
-    chunks = rows // CHUNK
+    chunks = rows // LOAD
     stay = lambda array: pltpu.with_memory_space_constraint(array, pltpu.HBM)
 
     tile = shape(4 * rows, TILE)
-    first, second, edge, kept, near, far, per_row = pl.pallas_call(
+    i32 = lambda *dims: jax.ShapeDtypeStruct(dims, jnp.int32)
+    tile = shape(4 * rows, TILE)
+    first, second, near, far, *inner = pl.pallas_call(
         block_kernel,
         in_specs=[hbm] * 7,
-        out_specs=[vmem] * 7,
+        out_specs=[vmem] * 14,
         out_shape=[
             tile,
             tile,
-            shape(2 * RAW * EDGE, TILE),
-            shape(14, 8, cols),
             shape(8, cols),
             shape(8, cols),
-            shape(8, TILE),
+            shape(rows, cols),
+            shape(2, rows, cols),
+            shape(rows, cols),
+            i32(rows, cols),
+            i32(rows, cols),
+            i32(rows * cols // TILE // TILE, TILE),
+            shape(4, 2, rows + 16, TILE),
+            shape(2, 2, rows + 8, TILE),
+            shape(2, 2, rows, TILE),
+            shape(rows, TILE),
         ],
         scratch_shapes=[
-            pltpu.VMEM((rows, cols), f32),
-            pltpu.VMEM((2, rows, cols), f32),
-            pltpu.VMEM((rows, cols), f32),
-            pltpu.VMEM((rows, cols), jnp.int32),
-            pltpu.VMEM((rows, cols), jnp.int32),
             pltpu.VMEM((1, rows), f32),
-            pltpu.VMEM((rows * cols // TILE // TILE, TILE), jnp.int32),
-            pltpu.VMEM((4, 2, rows + 16, TILE), f32),
-            pltpu.VMEM((2, 2, rows + 8, TILE), f32),
-            pltpu.VMEM((2, 2, rows, TILE), f32),
-            pltpu.VMEM((TILE, TILE), f32),
-            pltpu.VMEM((rows, TILE), f32),
             pltpu.VMEM((6, 2, rows, TILE), f32),
             pltpu.SemaphoreType.DMA((5, chunks)),
             pltpu.SemaphoreType.DMA((2,)),
@@ -550,6 +565,19 @@
     )(*map(stay, (density, velocity, energy, material, limiter, tile_shift, owners.reshape(-1, TILE))))
     from_near = lax.ppermute(first, "gx", near_pairs(gx))
     from_far = lax.ppermute(second, "gx", far_pairs(gx))
+    edge, kept, per_row = pl.pallas_call(
+        rows_kernel,
+        in_specs=[vmem] * 10,
+        out_specs=[vmem] * 3,
+        out_shape=[
+            shape(2 * RAW * EDGE, TILE),
+            shape(14, 8, cols),
+            shape(8, TILE),
+        ],
+        scratch_shapes=[pltpu.VMEM((rows, TILE), f32)],
+        compiler_params=params,
+        name="outer",
+    )(*inner)
     near = lax.ppermute(near, "gy", near_pairs(gy))
     far = lax.ppermute(far, "gy", far_pairs(gy))
 
@@ -579,7 +607,7 @@
         in_specs=[vmem] * 10,
         out_specs=hbm,
         out_shape=shape(4, planes, rows, cols),
-        scratch_shapes=[pltpu.VMEM((4, rows, cols), f32), pltpu.SemaphoreType.DMA((chunks,))],
+        scratch_shapes=[pltpu.VMEM((4, rows, cols), f32), pltpu.SemaphoreType.DMA((rows // CHUNK,))],
         compiler_params=params,
         name="merge",
     )(

time: 21.9 us -> 21.3 us (0.973)
  waiting for transfers between devices: 6.44 us -> 5.93 us
    ppermute x1, waiting for transfers between devices: 1.47 us -> 0.96 us  [on_device(): far = lax.ppermute(far, 'gy', far_pairs(gy))]
    pallas_call x1 -> x2, Pallas kernels: 3.07 us -> 3.2 us  [the longest x1 2.7 us: on_device(): pl.pallas_call(block_kernel, in_specs=[hbm] * 7, out_specs=[vmem] * 14, o...]
  transfers between devices with their start and end apart: 6 -> 6, of which waited for: 3 -> 3; matrix products, arithmetic and copies ran while one was open for 0% -> 0% of each run, Pallas kernels for 3% -> 6%
where the time goes in v4:
time: 21.3 us; the launch traced here: 21.2 us
  starting transfers between devices  10.2 us (48%)
  waiting for transfers between devices  5.93 us (28%)
  Pallas kernels  5.03 us (24%)
    ppermute x1, waiting for transfers between devices, on_device(): small_near = lax.ppermute(small_first, 'gx', near_pairs(gx))  3.63 us
    ppermute x1, starting transfers between devices, on_device(): from_far = lax.ppermute(second, 'gx', far_pairs(gx))  3.54 us
    ppermute x1, starting transfers between devices, on_device(): from_near = lax.ppermute(first, 'gx', near_pairs(gx))  3.06 us
    pallas_call x1, Pallas kernels, on_device(): pl.pallas_call(block_kernel, in_specs=[hbm] * 7, out_specs=[vmem] * 14, o...  2.7 us
    ppermute x1, starting transfers between devices, on_device(): small_far = lax.ppermute(small_second, 'gx', far_pairs(gx))  1.9 us
    ppermute x1, starting transfers between devices, on_device(): far = lax.ppermute(far, 'gy', far_pairs(gy))  1.6 us
    ppermute x1, waiting for transfers between devices, on_device(): small_far = lax.ppermute(small_second, 'gx', far_pairs(gx))  1.33 us
    pallas_call x1, Pallas kernels, on_device(): pl.pallas_call(merge_kernel, in_specs=[vmem] * 10, out_specs=hbm, out_sha...  1.16 us
  transfers between devices with their start and end apart: 6, of which 3 were waited for; matrix products, arithmetic and copies ran while one was open for 0% of the time, Pallas kernels for 6%

profile of v4, /device:TPU:0, one launch (start us, length us, event | category | flops | bytes accessed | tf_op | source)
XLA Modules:
  0.0 21.2 jit_solution(7223219452621798071)
XLA Ops:
  0.0 2.7 %block.1 = (f32[512,128]{1,0:T(8,128)S(1)}, f32[512,128]{1,0:T(8,128)S(1)}, f32[8,256]{1,0:T(8,128)S(1)}, f32[8,256]{1,0:T(8,128)S(1)}, f32[128,256]{1,0:T(8,128...) custom-call(f32[1,128,256]{2,1,0:T(8,128)} %rho_hbm.1, ...), custom_call_target="tpu_custom_call" | custom-call | tf_op jit(solution)/shard_map/block/pallas_call | solution.py:537
  2.7 3.1 %collective-permute-start = (f32[512,128]{1,0:T(8,128)S(1)}, f32[512,128]{1,0:T(8,128)S(1)}, u32[]{:S(2)}, u32[]{:S(2)}) collective-permute-start(f32[512,128]{1,0:T(8,128)S(1)} %get-tuple-element.25.first_ref), channel_id=1, source_target_pairs={{0,4},{4,0},{8,12},{12,8},{16,20},{20,16},{24,28},{28,24},{1,5},{5... | collective-permute-start | bytes 786440 | tf_op jit(solution)/shard_map/ppermute | solution.py:566
  5.8 3.5 %collective-permute-start.1 = (f32[512,128]{1,0:T(8,128)S(1)}, f32[512,128]{1,0:T(8,128)S(1)}, u32[]{:S(2)}, u32[]{:S(2)}) collective-permute-start(f32[512,128]{1,0:T(8,128)S(1)} %get-tuple-element.26.second_ref), channel_id=1, source_target_pairs={{4,8},{8,4},{12,16},{16,12},{20,24},{24,20},{28,0},{0,28},{5,9},{9... | collective-permute-start | bytes 786440 | tf_op jit(solution)/shard_map/ppermute | solution.py:567
  9.3 0.0 collective-permute-start.2
  9.3 1.6 %collective-permute-start.3 = (f32[8,256]{1,0:T(8,128)S(1)}, f32[8,256]{1,0:T(8,128)S(1)}, u32[]{:S(2)}, u32[]{:S(2)}) collective-permute-start(f32[8,256]{1,0:T(8,128)S(1)} %get-tuple-element.28), channel_id=1, source_target_pairs={{1,2},{2,1},{3,0},{0,3},{5,6},{6,5},{7,4},{4,7},{9,10},{10,9},{11,... | collective-permute-start | bytes 24584 | tf_op jit(solution)/shard_map/ppermute | solution.py:582
  10.9 0.5 %outer.1 = (f32[96,128]{1,0:T(8,128)S(1)}, f32[14,8,256]{2,1,0:T(8,128)S(1)}, f32[8,128]{1,0:T(8,128)S(1)}) custom-call(f32[128,256]{1,0:T(8,128)S(1)} %get-tuple-element.29.rho_ref, f32[2,128,256]{2,1,0:T(8,128)S(1)} %get-tuple-element.30.vel_ref, f32[128,256]{1,0:T(8,128)S(1)} %get-tuple-element.31.en_ref, s32[128,256]{1,0:T(8,128)S(1)} %get-tuple-element.32.mat_ref, ...), custom_call_target="tpu_custom_call" | custom-call | tf_op jit(solution)/shard_map/outer/pallas_call | solution.py:568
  11.4 0.0 collective-permute-done.2.near_ref
  11.4 1.0 %collective-permute-done.3.far_ref = f32[8,256]{1,0:T(8,128)S(1)} collective-permute-done((f32[8,256]{1,0:T(8,128)S(1)}, f32[8,256]{1,0:T(8,128)S(1)}, u32[]{:S(2)}, u32[]{:S(2)}) %collective-permute-start.3) | collective-permute-done | bytes 8224 | tf_op jit(solution)/shard_map/ppermute | solution.py:582
  12.4 0.4 %rim.1 = (f32[64,128]{1,0:T(8,128)S(1)}, f32[64,128]{1,0:T(8,128)S(1)}, f32[16,128]{1,0:T(8,128)S(1)}) custom-call(f32[8,256]{1,0:T(8,128)S(1)} %collective-permute-done.2.near_ref, f32[8,256]{1,0:T(8,128)S(1)} %collective-permute-done.3.far_ref, f32[14,8,256]{2,1,0:T(8,128)S(1)} %get-tuple-element.39.kept_ref, f32[96,128]{1,0:T(8,128)S(1)} %get-tuple-element.40.edge_ref), custom_call_target="tpu_custom_call" | custom-call | tf_op jit(solution)/shard_map/rim/pallas_call | solution.py:585
  12.8 0.1 collective-permute-start.4
  12.9 1.9 %collective-permute-start.5 = (f32[64,128]{1,0:T(8,128)S(1)}, f32[64,128]{1,0:T(8,128)S(1)}, u32[]{:S(2)}, u32[]{:S(2)}) collective-permute-start(f32[64,128]{1,0:T(8,128)S(1)} %get-tuple-element.42.rim_second_ref), channel_id=1, source_target_pairs={{4,8},{8,4},{12,16},{16,12},{20,24},{24,20},{28,0},{0,28},{5,9},{9... | collective-permute-start | bytes 98312 | tf_op jit(solution)/shard_map/ppermute | solution.py:594
  14.8 3.6 %collective-permute-done.4.from_near_ref.rim_near_ref = f32[64,128]{1,0:T(8,128)S(1)} collective-permute-done((f32[64,128]{1,0:T(8,128)S(1)}, f32[64,128]{1,0:T(8,128)S(1)}, u32[]{:S(2)}, u32[]{:S(2)}) %collective-permute-start.4) | collective-permute-done | bytes 32800 | tf_op jit(solution)/shard_map/ppermute | solution.py:593
  18.4 1.3 %collective-permute-done.5.from_far_ref.rim_far_ref = f32[64,128]{1,0:T(8,128)S(1)} collective-permute-done((f32[64,128]{1,0:T(8,128)S(1)}, f32[64,128]{1,0:T(8,128)S(1)}, u32[]{:S(2)}, u32[]{:S(2)}) %collective-permute-start.5) | collective-permute-done | bytes 32800 | tf_op jit(solution)/shard_map/ppermute | solution.py:594
  19.7 0.3 %edge.1.patch_ref = f32[128,128]{1,0:T(8,128)S(1)} custom-call(f32[96,128]{1,0:T(8,128)S(1)} %get-tuple-element.40.edge_ref, f32[16,128]{1,0:T(8,128)S(1)} %get-tuple-element.43.corner_ref, f32[64,128]{1,0:T(8,128)S(1)} %collective-permute-done.4.from_near_ref.rim_near_ref, f32[64,128]{1,0:T(8,128)S(1)} %collective-permute-done.5.from_far_ref.rim_far_ref, ...), custom_call_target="tpu_custom_call" | custom-call | tf_op jit(solution)/shard_map/edge/pallas_call | solution.py:596
  20.0 0.0 collective-permute-done.from_near_ref
  20.0 0.0 collective-permute-done.1.from_far_ref
  20.0 1.2 %merge.1 = f32[4,1,128,256]{3,2,1,0:T(8,128)} custom-call(f32[512,128]{1,0:T(8,128)S(1)} %get-tuple-element.25.first_ref, f32[512,128]{1,0:T(8,128)S(1)} %get-tuple-element.26.second_ref, f32[512,128]{1,0:T(8,128)S(1)} %collective-permute-done.from_near_ref, f32[512,128]{1,0:T(8,128)S(1)} %collective-permute-done.1.from_far_ref, ...), custom_call_target="tpu_custom_call" | custom-call | tf_op jit(solution)/shard_map/merge/pallas_call | solution.py:605
Async XLA Ops:
  2.7 17.3 %collective-permute-start = (f32[512,128]{1,0:T(8,128)S(1)}, f32[512,128]{1,0:T(8,128)S(1)}, u32[]{:S(2)}, u32[]{:S(2)}) collective-permute-start(f32[512,128]{1,0:T(8,128)S(1)} %get-tuple-element.25.first_ref), channel_id=1, source_target_pairs={{0,4},{4,0},{8,12},{12,8},{16,20},{20,16},{24,28},{28,24},{1,5},{5... | collective-permute-start | bytes 786440 | tf_op jit(solution)/shard_map/ppermute | solution.py:566
  5.8 14.3 %collective-permute-start.1 = (f32[512,128]{1,0:T(8,128)S(1)}, f32[512,128]{1,0:T(8,128)S(1)}, u32[]{:S(2)}, u32[]{:S(2)}) collective-permute-start(f32[512,128]{1,0:T(8,128)S(1)} %get-tuple-element.26.second_ref), channel_id=1, source_target_pairs={{4,8},{8,4},{12,16},{16,12},{20,24},{24,20},{28,0},{0,28},{5,9},{9... | collective-permute-start | bytes 786440 | tf_op jit(solution)/shard_map/ppermute | solution.py:567
  9.3 2.1 %collective-permute-start.2 = (f32[8,256]{1,0:T(8,128)S(1)}, f32[8,256]{1,0:T(8,128)S(1)}, u32[]{:S(2)}, u32[]{:S(2)}) collective-permute-start(f32[8,256]{1,0:T(8,128)S(1)} %get-tuple-element.27), channel_id=1, source_target_pairs={{0,1},{1,0},{2,3},{3,2},{4,5},{5,4},{6,7},{7,6},{8,9},{9,8},{10,11... | collective-permute-start | bytes 24584 | tf_op jit(solution)/shard_map/ppermute | solution.py:581
  9.3 3.1 %collective-permute-start.3 = (f32[8,256]{1,0:T(8,128)S(1)}, f32[8,256]{1,0:T(8,128)S(1)}, u32[]{:S(2)}, u32[]{:S(2)}) collective-permute-start(f32[8,256]{1,0:T(8,128)S(1)} %get-tuple-element.28), channel_id=1, source_target_pairs={{1,2},{2,1},{3,0},{0,3},{5,6},{6,5},{7,4},{4,7},{9,10},{10,9},{11,... | collective-permute-start | bytes 24584 | tf_op jit(solution)/shard_map/ppermute | solution.py:582
  12.8 5.6 %collective-permute-start.4 = (f32[64,128]{1,0:T(8,128)S(1)}, f32[64,128]{1,0:T(8,128)S(1)}, u32[]{:S(2)}, u32[]{:S(2)}) collective-permute-start(f32[64,128]{1,0:T(8,128)S(1)} %get-tuple-element.41.rim_first_ref), channel_id=1, source_target_pairs={{0,4},{4,0},{8,12},{12,8},{16,20},{20,16},{24,28},{28,24},{1,5},{5... | collective-permute-start | bytes 98312 | tf_op jit(solution)/shard_map/ppermute | solution.py:593
  12.9 6.9 %collective-permute-start.5 = (f32[64,128]{1,0:T(8,128)S(1)}, f32[64,128]{1,0:T(8,128)S(1)}, u32[]{:S(2)}, u32[]{:S(2)}) collective-permute-start(f32[64,128]{1,0:T(8,128)S(1)} %get-tuple-element.42.rim_second_ref), channel_id=1, source_target_pairs={{4,8},{8,4},{12,16},{16,12},{20,24},{24,20},{28,0},{0,28},{5,9},{9... | collective-permute-start | bytes 98312 | tf_op jit(solution)/shard_map/ppermute | solution.py:594

commit v5 on v4

--- a/solution.py
+++ b/solution.py
@@ -11,11 +11,12 @@
 STEP = 8
 BLOCK = (8, 8, 16, 8)
 MERGE = 8
-EDGES = 4
+EDGES = 8
 LOAD = 64
 CHUNK = 64
 VMEM_LIMIT = 8 << 20
-EDGE = 8
+EDGE = 5
+SPAN = 24
 RAW = 6
 
 
@@ -414,23 +415,22 @@
         second_ref[spot, :] = jnp.where(even_x, left_edge, right_edge)
 
 
-def edge_kernel(edge_ref, corner_ref, from_near_ref, from_far_ref, row_ref, patch_ref):
+def edge_kernel(edge_ref, corner_ref, from_near_ref, from_far_ref, row_ref, patch_ref, window_ref):
     rows = patch_ref.shape[0]
     even_x = lax.axis_index("gx") % 2 == 0
-    span = 4 * EDGE
+    span = SPAN
 
     def window(k):
         spot = slice(8 + k * EDGE, 8 + (k + 1) * EDGE)
         own, at = (edge_ref, 2 * k * EDGE) if k < RAW else (corner_ref, 0)
-        return jnp.concatenate(
-            [
-                jnp.where(even_x, from_far_ref[spot, :], from_near_ref[spot, :]),
-                own[at + EDGE : at + 2 * EDGE, :],
-                own[at : at + EDGE, :],
-                jnp.where(even_x, from_near_ref[spot, :], from_far_ref[spot, :]),
-            ],
-            axis=0,
-        )
+        right_end, left_end = own[at : at + EDGE, :], own[at + EDGE : at + 2 * EDGE, :]
+        near, far = from_near_ref[spot, :], from_far_ref[spot, :]
+        window_ref[k, 0:EDGE, :] = jnp.where(even_x, far, near)
+        window_ref[k, EDGE : 2 * EDGE, :] = left_end
+        window_ref[k, 2 * EDGE : 3 * EDGE, :] = right_end
+        window_ref[k, 3 * EDGE : 4 * EDGE, :] = jnp.where(even_x, near, far)
+        window_ref[k, 4 * EDGE : span, :] = right_end[0 : span - 4 * EDGE, :]
+        return window_ref[k, :, :]
 
     left = lambda a: pltpu.roll(a, 1, 0)
     right = lambda a: pltpu.roll(a, span - 1, 0)
@@ -449,6 +449,7 @@
     )
     weights = next_weights(row_ref[0:1, :], ends_left, ends_right)
     fields = [remapped_field(q, scale, 2.0 * lim + 2.0, weights, left, right) for q in conserved]
+    fields.append(jnp.zeros((TILE - 4 * span, rows), jnp.float32))
     patch_ref[...] = jnp.concatenate(fields, axis=0).T
 
 
@@ -458,7 +459,7 @@
     row_ref, out_hbm, out_ref, sems,
 ):
     rows = out_ref.shape[1]
-    span = 4 * EDGE
+    span = SPAN
     chunks, inner = rows // CHUNK, CHUNK // STEP
     even_x = lax.axis_index("gx") % 2 == 0
     to_left, to_right = row_ref[1:2, :], row_ref[2:3, :]
@@ -598,6 +599,7 @@
         in_specs=[vmem] * 5,
         out_specs=vmem,
         out_shape=shape(rows, TILE),
+        scratch_shapes=[pltpu.VMEM((RAW + 1, SPAN, rows), f32)],
         compiler_params=params,
         name="edge",
     )(edge, corner, small_near, small_far, per_row)

time: 21.3 us -> 21.2 us (level)
  transfers between devices with their start and end apart: 6 -> 6, of which waited for: 3 -> 3; matrix products, arithmetic and copies ran while one was open for 0% -> 0% of each run, Pallas kernels for 6% -> 5%
where the time goes in v5:
time: 21.2 us; the launch traced here: 21 us
  starting transfers between devices  10.2 us (48%)
  waiting for transfers between devices  5.91 us (28%)
  Pallas kernels  4.88 us (23%)
    ppermute x1, starting transfers between devices, on_device(): from_far = lax.ppermute(second, 'gx', far_pairs(gx))  3.54 us
    ppermute x1, waiting for transfers between devices, on_device(): small_near = lax.ppermute(small_first, 'gx', near_pairs(gx))  3.45 us
    ppermute x1, starting transfers between devices, on_device(): from_near = lax.ppermute(first, 'gx', near_pairs(gx))  3.06 us
    pallas_call x1, Pallas kernels, on_device(): pl.pallas_call(block_kernel, in_specs=[hbm] * 7, out_specs=[vmem] * 14, o...  2.72 us
    ppermute x1, starting transfers between devices, on_device(): small_far = lax.ppermute(small_second, 'gx', far_pairs(gx))  1.9 us
    ppermute x1, starting transfers between devices, on_device(): far = lax.ppermute(far, 'gy', far_pairs(gy))  1.6 us
    ppermute x1, waiting for transfers between devices, on_device(): small_far = lax.ppermute(small_second, 'gx', far_pairs(gx))  1.34 us
    pallas_call x1, Pallas kernels, on_device(): pl.pallas_call(merge_kernel, in_specs=[vmem] * 10, out_specs=hbm, out_sha...  1.15 us
  transfers between devices with their start and end apart: 6, of which 3 were waited for; matrix products, arithmetic and copies ran while one was open for 0% of the time, Pallas kernels for 5%

profile of v5, /device:TPU:0, one launch (start us, length us, event | category | flops | bytes accessed | tf_op | source)
XLA Modules:
  0.0 21.0 jit_solution(6764749713343355868)
XLA Ops:
  0.0 2.7 %block.1 = (f32[512,128]{1,0:T(8,128)S(1)}, f32[512,128]{1,0:T(8,128)S(1)}, f32[8,256]{1,0:T(8,128)S(1)}, f32[8,256]{1,0:T(8,128)S(1)}, f32[128,256]{1,0:T(8,128...) custom-call(f32[1,128,256]{2,1,0:T(8,128)} %rho_hbm.1, ...), custom_call_target="tpu_custom_call" | custom-call | tf_op jit(solution)/shard_map/block/pallas_call | solution.py:538
  2.7 3.1 %collective-permute-start = (f32[512,128]{1,0:T(8,128)S(1)}, f32[512,128]{1,0:T(8,128)S(1)}, u32[]{:S(2)}, u32[]{:S(2)}) collective-permute-start(f32[512,128]{1,0:T(8,128)S(1)} %get-tuple-element.25.first_ref), channel_id=1, source_target_pairs={{0,4},{4,0},{8,12},{12,8},{16,20},{20,16},{24,28},{28,24},{1,5},{5... | collective-permute-start | bytes 786440 | tf_op jit(solution)/shard_map/ppermute | solution.py:567
  5.8 3.5 %collective-permute-start.1 = (f32[512,128]{1,0:T(8,128)S(1)}, f32[512,128]{1,0:T(8,128)S(1)}, u32[]{:S(2)}, u32[]{:S(2)}) collective-permute-start(f32[512,128]{1,0:T(8,128)S(1)} %get-tuple-element.26.second_ref), channel_id=1, source_target_pairs={{4,8},{8,4},{12,16},{16,12},{20,24},{24,20},{28,0},{0,28},{5,9},{9... | collective-permute-start | bytes 786440 | tf_op jit(solution)/shard_map/ppermute | solution.py:568
  9.3 0.0 collective-permute-start.2
  9.3 1.6 %collective-permute-start.3 = (f32[8,256]{1,0:T(8,128)S(1)}, f32[8,256]{1,0:T(8,128)S(1)}, u32[]{:S(2)}, u32[]{:S(2)}) collective-permute-start(f32[8,256]{1,0:T(8,128)S(1)} %get-tuple-element.28), channel_id=1, source_target_pairs={{1,2},{2,1},{3,0},{0,3},{5,6},{6,5},{7,4},{4,7},{9,10},{10,9},{11,... | collective-permute-start | bytes 24584 | tf_op jit(solution)/shard_map/ppermute | solution.py:583
  10.9 0.3 %outer.1 = (f32[60,128]{1,0:T(8,128)S(1)}, f32[14,8,256]{2,1,0:T(8,128)S(1)}, f32[8,128]{1,0:T(8,128)S(1)}) custom-call(f32[128,256]{1,0:T(8,128)S(1)} %get-tuple-element.29.rho_ref, f32[2,128,256]{2,1,0:T(8,128)S(1)} %get-tuple-element.30.vel_ref, f32[128,256]{1,0:T(8,128)S(1)} %get-tuple-element.31.en_ref, s32[128,256]{1,0:T(8,128)S(1)} %get-tuple-element.32.mat_ref, ...), custom_call_target="tpu_custom_call" | custom-call | tf_op jit(solution)/shard_map/outer/pallas_call | solution.py:569
  11.3 0.0 collective-permute-done.2.near_ref
  11.3 1.1 %collective-permute-done.3.far_ref = f32[8,256]{1,0:T(8,128)S(1)} collective-permute-done((f32[8,256]{1,0:T(8,128)S(1)}, f32[8,256]{1,0:T(8,128)S(1)}, u32[]{:S(2)}, u32[]{:S(2)}) %collective-permute-start.3) | collective-permute-done | bytes 8224 | tf_op jit(solution)/shard_map/ppermute | solution.py:583
  12.4 0.4 %rim.1 = (f32[43,128]{1,0:T(8,128)S(1)}, f32[43,128]{1,0:T(8,128)S(1)}, f32[10,128]{1,0:T(8,128)S(1)}) custom-call(f32[8,256]{1,0:T(8,128)S(1)} %collective-permute-done.2.near_ref, f32[8,256]{1,0:T(8,128)S(1)} %collective-permute-done.3.far_ref, f32[14,8,256]{2,1,0:T(8,128)S(1)} %get-tuple-element.39.kept_ref, f32[60,128]{1,0:T(8,128)S(1)} %get-tuple-element.40.edge_ref), custom_call_target="tpu_custom_call" | custom-call | tf_op jit(solution)/shard_map/rim/pallas_call | solution.py:586
  12.8 0.1 collective-permute-start.4
  12.9 1.9 %collective-permute-start.5 = (f32[43,128]{1,0:T(8,128)S(1)}, f32[43,128]{1,0:T(8,128)S(1)}, u32[]{:S(2)}, u32[]{:S(2)}) collective-permute-start(f32[43,128]{1,0:T(8,128)S(1)} %get-tuple-element.42.rim_second_ref), channel_id=1, source_target_pairs={{4,8},{8,4},{12,16},{16,12},{20,24},{24,20},{28,0},{0,28},{5,9},{9... | collective-permute-start | bytes 66056 | tf_op jit(solution)/shard_map/ppermute | solution.py:595
  14.8 3.4 %collective-permute-done.4.from_near_ref.rim_near_ref = f32[43,128]{1,0:T(8,128)S(1)} collective-permute-done((f32[43,128]{1,0:T(8,128)S(1)}, f32[43,128]{1,0:T(8,128)S(1)}, u32[]{:S(2)}, u32[]{:S(2)}) %collective-permute-start.4) | collective-permute-done | bytes 22048 | tf_op jit(solution)/shard_map/ppermute | solution.py:594
  18.2 1.3 %collective-permute-done.5.from_far_ref.rim_far_ref = f32[43,128]{1,0:T(8,128)S(1)} collective-permute-done((f32[43,128]{1,0:T(8,128)S(1)}, f32[43,128]{1,0:T(8,128)S(1)}, u32[]{:S(2)}, u32[]{:S(2)}) %collective-permute-start.5) | collective-permute-done | bytes 22048 | tf_op jit(solution)/shard_map/ppermute | solution.py:595
  19.6 0.3 %edge.1.patch_ref = f32[128,128]{1,0:T(8,128)S(1)} custom-call(f32[60,128]{1,0:T(8,128)S(1)} %get-tuple-element.40.edge_ref, f32[10,128]{1,0:T(8,128)S(1)} %get-tuple-element.43.corner_ref, f32[43,128]{1,0:T(8,128)S(1)} %collective-permute-done.4.from_near_ref.rim_near_ref, f32[43,128]{1,0:T(8,128)S(1)} %collective-permute-done.5.from_far_ref.rim_far_ref, ...), custom_call_target="tpu_custom_call" | custom-call | tf_op jit(solution)/shard_map/edge/pallas_call | solution.py:597
  19.9 0.0 collective-permute-done.from_near_ref
  19.9 0.0 collective-permute-done.1.from_far_ref
  19.9 1.2 %merge.1 = f32[4,1,128,256]{3,2,1,0:T(8,128)} custom-call(f32[512,128]{1,0:T(8,128)S(1)} %get-tuple-element.25.first_ref, f32[512,128]{1,0:T(8,128)S(1)} %get-tuple-element.26.second_ref, f32[512,128]{1,0:T(8,128)S(1)} %collective-permute-done.from_near_ref, f32[512,128]{1,0:T(8,128)S(1)} %collective-permute-done.1.from_far_ref, ...), custom_call_target="tpu_custom_call" | custom-call | tf_op jit(solution)/shard_map/merge/pallas_call | solution.py:607
Async XLA Ops:
  2.7 17.1 %collective-permute-start = (f32[512,128]{1,0:T(8,128)S(1)}, f32[512,128]{1,0:T(8,128)S(1)}, u32[]{:S(2)}, u32[]{:S(2)}) collective-permute-start(f32[512,128]{1,0:T(8,128)S(1)} %get-tuple-element.25.first_ref), channel_id=1, source_target_pairs={{0,4},{4,0},{8,12},{12,8},{16,20},{20,16},{24,28},{28,24},{1,5},{5... | collective-permute-start | bytes 786440 | tf_op jit(solution)/shard_map/ppermute | solution.py:567
  5.8 14.1 %collective-permute-start.1 = (f32[512,128]{1,0:T(8,128)S(1)}, f32[512,128]{1,0:T(8,128)S(1)}, u32[]{:S(2)}, u32[]{:S(2)}) collective-permute-start(f32[512,128]{1,0:T(8,128)S(1)} %get-tuple-element.26.second_ref), channel_id=1, source_target_pairs={{4,8},{8,4},{12,16},{16,12},{20,24},{24,20},{28,0},{0,28},{5,9},{9... | collective-permute-start | bytes 786440 | tf_op jit(solution)/shard_map/ppermute | solution.py:568
  9.3 2.0 %collective-permute-start.2 = (f32[8,256]{1,0:T(8,128)S(1)}, f32[8,256]{1,0:T(8,128)S(1)}, u32[]{:S(2)}, u32[]{:S(2)}) collective-permute-start(f32[8,256]{1,0:T(8,128)S(1)} %get-tuple-element.27), channel_id=1, source_target_pairs={{0,1},{1,0},{2,3},{3,2},{4,5},{5,4},{6,7},{7,6},{8,9},{9,8},{10,11... | collective-permute-start | bytes 24584 | tf_op jit(solution)/shard_map/ppermute | solution.py:582
  9.3 3.1 %collective-permute-start.3 = (f32[8,256]{1,0:T(8,128)S(1)}, f32[8,256]{1,0:T(8,128)S(1)}, u32[]{:S(2)}, u32[]{:S(2)}) collective-permute-start(f32[8,256]{1,0:T(8,128)S(1)} %get-tuple-element.28), channel_id=1, source_target_pairs={{1,2},{2,1},{3,0},{0,3},{5,6},{6,5},{7,4},{4,7},{9,10},{10,9},{11,... | collective-permute-start | bytes 24584 | tf_op jit(solution)/shard_map/ppermute | solution.py:583
  12.8 5.4 %collective-permute-start.4 = (f32[43,128]{1,0:T(8,128)S(1)}, f32[43,128]{1,0:T(8,128)S(1)}, u32[]{:S(2)}, u32[]{:S(2)}) collective-permute-start(f32[43,128]{1,0:T(8,128)S(1)} %get-tuple-element.41.rim_first_ref), channel_id=1, source_target_pairs={{0,4},{4,0},{8,12},{12,8},{16,20},{20,16},{24,28},{28,24},{1,5},{5... | collective-permute-start | bytes 66056 | tf_op jit(solution)/shard_map/ppermute | solution.py:594
  12.9 6.7 %collective-permute-start.5 = (f32[43,128]{1,0:T(8,128)S(1)}, f32[43,128]{1,0:T(8,128)S(1)}, u32[]{:S(2)}, u32[]{:S(2)}) collective-permute-start(f32[43,128]{1,0:T(8,128)S(1)} %get-tuple-element.42.rim_second_ref), channel_id=1, source_target_pairs={{4,8},{8,4},{12,16},{16,12},{20,24},{24,20},{28,0},{0,28},{5,9},{9... | collective-permute-start | bytes 66056 | tf_op jit(solution)/shard_map/ppermute | solution.py:595
